TPU v7x, 128 devices: a whole 4x4x4 slice. The times are simulated.
128 devices in a mesh: state: 32 (over x, y, core), mem: 4 (over z).
Axes of the slice: x: 4, y: 4, z: 4, core: 2. Of those that a mesh axis runs over, the one named last changes fastest.
Arguments:
- ensemble: bfloat16 [80, 1048576], P('mem', 'state'), may hold values from -6 to 6
- weights: bfloat16 [8192, 12, 128], P('state'), may hold values from 0 to 0.14941406
- seg_obs: int32 [8192, 12], P('state'), may hold values from 0 to 65535, as said below
- observed: float32 [65536], replicated, may hold values from -180 to 180
- inv_var: float32 [65536], replicated, may hold values from 0.0001 to 0.001
Outputs:
- analysis: bfloat16 [80, 1048576], P('mem', 'state')
Inputs may be any that keep to these rules, and one draw needn't show every extreme that they name: seg_obs names the observation that a slot's arc segment contributes to. Of the 3072 slots of the tiles of one index of state, exactly 96 name observations in each aligned block of 2048 observations; an observation may have any number of slots, or none.
All inputs are finite; a program needn't handle non-finite values.
Results may differ from a plain program's by a relative error of at most 0.0051.
Values may be sent and summed in bfloat16 or wider, within the bound.
A program may use at most 128 MiB of HBM per device.

v0:
```python
import math

import jax
import jax.numpy as jnp
from jax import lax
from jax.sharding import PartitionSpec as P

ITERS = 14


def sent_together(arrays, axis, split_dim, concat_dim, along):
    widths = [math.prod(a.shape[along:]) for a in arrays]
    both = jnp.concatenate(
        [a.reshape(*a.shape[:along], w) for a, w in zip(arrays, widths)], axis=along
    )
    out = lax.all_to_all(both, axis, split_axis=split_dim, concat_axis=concat_dim, tiled=True)
    parts = jnp.split(out, [sum(widths[:k]) for k in range(1, len(widths))], axis=along)
    return tuple((b.reshape(*out.shape[:along], *a.shape[along:]) for a, b in zip(arrays, parts)))


def copy_for_each(x, axis):
    peers = lax.axis_size(axis)
    return lax.all_to_all(jnp.broadcast_to(x[None], (peers, *x.shape)), axis, 0, 0, tiled=True)


def taken_together(x, axis):
    everything = copy_for_each(x, axis)
    return jnp.sum(everything, axis=0)


def in_one(arrays, axis):
    ends = [0]
    for a in arrays:
        ends.append(ends[-1] + a.size)
    subtotal = taken_together(jnp.concatenate([a.ravel() for a in arrays]), axis)
    return tuple((subtotal[b:e].reshape(a.shape) for a, b, e in zip(arrays, ends, ends[1:])))


def transform(gram, pull, members):
    identity = jnp.eye(members, dtype=jnp.float32)
    system = (members - 1.0) * identity + gram
    scaling = jnp.sqrt(jnp.sum(system * system))
    ynow = system / scaling
    znow = identity
    for step in range(ITERS):
        correct = 1.5 * identity - 0.5 * jnp.dot(znow, ynow, precision=lax.Precision.HIGHEST)
        ynow = jnp.dot(ynow, correct, precision=lax.Precision.HIGHEST)
        znow = jnp.dot(correct, znow, precision=lax.Precision.HIGHEST)
    root = znow / jnp.sqrt(scaling)
    shift = jnp.dot(
        root, jnp.dot(root, pull, precision=lax.Precision.HIGHEST), precision=lax.Precision.HIGHEST
    )
    mixed = shift[:, None] + math.sqrt(members - 1.0) * root
    mixed = mixed + (1.0 - jnp.sum(mixed, axis=0, keepdims=True)) / members
    return mixed.astype(jnp.bfloat16)


def statistics(everyone, obs_here, var_here, members):
    mean_obs = jnp.sum(everyone, axis=0) / members
    anomaly = everyone - mean_obs
    weighted = anomaly * var_here
    gram = jnp.dot(weighted, anomaly.T, precision=lax.Precision.HIGHEST)
    pull = jnp.dot(weighted, obs_here - mean_obs, precision=lax.Precision.HIGHEST)
    return (gram, pull)


def gather_members(shares):
    return lax.all_gather(shares.astype(jnp.bfloat16), "mem", axis=0, tiled=True).astype(
        jnp.float32
    )


def per_device(ensemble, weights, seg_obs, observed, inv_var):
    own_members, own_cells = ensemble.shape
    own_tiles, own_slots, tile_width = weights.shape
    obs_count = observed.shape[0]
    all_members = own_members * lax.axis_size("mem")
    blocks = ensemble.reshape(own_members, own_tiles, tile_width)
    values = jnp.einsum("ktc,tjc->tjk", blocks, weights, preferred_element_type=jnp.float32)
    values = values.reshape(own_tiles * own_slots, own_members)
    slot_ids = seg_obs.reshape(-1)
    share_width = obs_count // lax.axis_size("state")
    owner = slot_ids // share_width
    order = jnp.argsort(owner, stable=True)
    sorted_values = values[order]
    local_place = (slot_ids[order] % share_width).astype(jnp.float32)
    arrived, arrived_place = sent_together((sorted_values, local_place), "state", 0, 0, 1)
    landed = jax.ops.segment_sum(arrived, arrived_place.astype(jnp.int32), num_segments=share_width)
    shares = landed.T
    begin_at = lax.axis_index("state") * share_width
    obs_here = lax.dynamic_slice_in_dim(observed, begin_at, share_width)
    var_here = lax.dynamic_slice_in_dim(inv_var, begin_at, share_width)
    everyone = gather_members(shares)
    gram, pull = statistics(everyone, obs_here, var_here, all_members)
    gram, pull = in_one((gram, pull), "state")
    mixing = transform(gram, pull, all_members)
    regrouped = lax.all_to_all(ensemble, "mem", split_axis=1, concat_axis=0, tiled=True)
    updated = jnp.einsum("jk,js->ks", mixing, regrouped, preferred_element_type=jnp.float32).astype(
        jnp.bfloat16
    )
    return lax.all_to_all(updated, "mem", split_axis=0, concat_axis=1, tiled=True)


def solution(mesh):
    return jax.shard_map(
        per_device,
        mesh=mesh,
        in_specs=(P("mem", "state"), P("state", None, None), P("state", None), P(), P()),
        out_specs=P("mem", "state"),
        check_vma=False,
    )
```

profile of v0, /device:TPU:1, one launch (start us, length us, event | category | flops | bytes accessed | tf_op | source)
XLA Modules:
  0.0 159.3 jit_solution(11215360231634751820)
XLA Ops:
  0.0 0.8 copy.66
  1.0 5.8 %sort.17 = (s32[3072]{0:T(1024)}, s32[3072]{0:T(1024)S(1)}) sort(s32[3072]{0:T(1024)S(1)} %add_select_fusion.1, s32[3072]{0:T(1024)S(1)} %iota.88), dimensions={0}, to_apply=%region_0.1 | sort | flops 36864 | bytes 49152 | tf_op jit(solution)/shard_map/jit(argsort)/sort | solution.py:84
  6.7 17.4 %gather_fusion.1 = s32[3072]{0:T(1024)S(1)} fusion(s32[3072]{0:T(1024)S(1)} %reshape.116, s32[3072]{0:T(1024)S(1)} %fusion.37), kind=kCustom, calls=%fused_computation.1 | custom fusion | bytes 36864 | tf_op jit(solution)/shard_map/gather | solution.py:86
  24.3 0.3 copy.80
  24.7 1.0 copy-done.2
  25.7 2.7 %fusion = f32[256,12,20]{2,1,0:T(8,128)} fusion(bf16[20,256,128]{2,1,0:T(8,128)(2,1)S(1)} %slice.22, bf16[256,12,128]{2,0,1:T(8,128)(2,1)S(1)} %copy-done.2), kind=kOutput, calls=%fused_computation.4 | convolution fusion | flops 15728640 | bytes 2342912 | tf_op jit(solution)/shard_map/ktc,tjc->tjk/dot_general | solution.py:79
  28.4 1.6 %reshape.154 = f32[3072,20]{1,0:T(8,128)S(1)} reshape(f32[256,12,20]{2,1,0:T(8,128)} %fusion) | data formatting | bytes 491520 | tf_op jit(solution)/shard_map/reshape | solution.py:80
  30.0 8.1 %gather_fusion = f32[3072,20]{1,0:T(8,128)S(1)} fusion(f32[3072,20]{1,0:T(8,128)S(1)} %reshape.154, s32[3072]{0:T(1024)S(1)} %fusion.37), kind=kCustom, calls=%fused_computation | custom fusion | bytes 503808 | tf_op jit(solution)/shard_map/gather | solution.py:85
  38.2 0.5 copy.68
  38.7 0.8 pad_maximum_fusion
  39.5 8.6 %all-to-all-start = ((f32[32,96,21]{1,2,0:T(8,128)}), f32[32,96,21]{1,2,0:T(8,128)S(1)}, u32[]{:S(2)}, u32[]{:S(2)}) async-start(f32[32,96,21]{1,2,0:T(8,128)} %pad_maximum_fusion), calls=%async_computation | async-start | bytes 786432 | tf_op jit(solution)/shard_map/all_to_all | solution.py:16
  48.1 2.1 %all_to_all.41 = bf16[20,4,8192]{2,1,0:T(4,128)(2,1)S(1)} reshape(bf16[20,32768]{1,0:T(8,128)(2,1)S(1)} %copy-done.1) | data formatting | bytes 2621440 | tf_op jit(solution)/shard_map/all_to_all | solution.py:97
  50.2 1.9 %copy.74 = bf16[20,4,8192]{2,0,1:T(8,128)(2,1)} copy(bf16[20,4,8192]{2,1,0:T(4,128)(2,1)S(1)} %all_to_all.41) | data formatting | bytes 2621440 | tf_op jit(solution)/shard_map/all_to_all | solution.py:97
  52.1 0.7 dynamic_slice.6
  52.8 5.6 %all-to-all-done = f32[32,96,21]{1,2,0:T(8,128)S(1)} async-done(((f32[32,96,21]{1,2,0:T(8,128)}), f32[32,96,21]{1,2,0:T(8,128)S(1)}, u32[]{:S(2)}, u32[]{:S(2)}) %all-to-all-start) | async-done | bytes 258080 | tf_op jit(solution)/shard_map/all_to_all | solution.py:16
  58.3 5.0 %all-to-all-start.2 = ((bf16[20,4,8192]{2,0,1:T(8,128)(2,1)}), bf16[20,4,8192]{2,0,1:T(8,128)(2,1)S(1)}, u32[]{:S(2)}, u32[]{:S(2)}) async-start(bf16[20,4,8192]{2,0,1:T(8,128)(2,1)} %copy.74), calls=%async_computation.2 | async-start | bytes 3145728 | tf_op jit(solution)/shard_map/all_to_all | solution.py:97
  63.4 0.2 all_to_all.39
  63.7 1.7 %copy.71 = f32[3072,20]{1,0:T(8,128)} copy(f32[3072,20]{0,1:T(8,128)S(1)} %bitcast.118) | data formatting | bytes 491520 | tf_op jit(solution)/shard_map/split | solution.py:17
  65.4 17.5 %scatter_custom_fusion = f32[2048,20]{1,0:T(8,128)S(1)} fusion(s32[3072]{0:T(1024)S(1)} %bitcast.121, f32[3072,20]{1,0:T(8,128)} %copy.71, f32[]{:T(128)} %constant.44.clone.1), kind=kCustom, calls=%fused_computation.45 | custom fusion | flops 61440 | bytes 164352 | tf_op jit(solution)/shard_map/scatter-add | solution.py:88
  82.9 0.2 copy.72
  83.1 10.9 %all-gather = bf16[4,20,2048]{2,1,0:T(8,128)(2,1)S(1)} all-gather(bf16[1,20,2048]{2,1,0:T(8,128)(2,1)S(1)} %copy.72), channel_id=1, replica_groups=mesh['state'=32,'mem'=4] {'mem'}, dimensions={0}, use_global_device_ids=true | all-gather | bytes 409600 | tf_op jit(solution)/shard_map/all_gather | solution.py:68
  94.2 0.7 broadcast_multiply_fusion
  94.9 0.7 fusion.18
  95.7 0.6 convolution_bitcast_fusion.2
  96.3 1.3 broadcast_in_dim.8
  97.7 7.1 %all-to-all-start.1 = ((f32[32,1,6480]{2,1,0:T(1,128)}), f32[32,1,6480]{2,1,0:T(1,128)}, u32[]{:S(2)}, u32[]{:S(2)}) async-start(f32[32,1,6480]{2,1,0:T(1,128)} %broadcast_in_dim.8), calls=%async_computation.1 | async-start | bytes 1671168 | tf_op jit(solution)/shard_map/all_to_all | solution.py:23
  104.9 0.4 all_to_all.44
  105.3 14.4 %all-to-all-done.1 = f32[32,1,6480]{2,1,0:T(1,128)} async-done(((f32[32,1,6480]{2,1,0:T(1,128)}), f32[32,1,6480]{2,1,0:T(1,128)}, u32[]{:S(2)}, u32[]{:S(2)}) %all-to-all-start.1) | async-done | bytes 829472 | tf_op jit(solution)/shard_map/all_to_all | solution.py:23
  119.7 1.6 %reduce_sum.37 = f32[6480]{0:T(1024)S(1)} reduce(f32[32,1,6480]{2,1,0:T(1,128)} %all-to-all-done.1, f32[]{:T(128)} %constant.44.clone.1), dimensions={0,1}, to_apply=%region_3.4 | reduce | flops 200880 | bytes 855364 | tf_op jit(solution)/shard_map/reduce_sum | solution.py:28
  121.3 0.6 multiply_reduce_fusion
  122.9 0.2 fusion.39
  123.2 0.2 fusion.14
  123.7 0.2 fusion.13
  123.9 0.2 fusion.48
  124.1 0.2 fusion.47
  124.3 0.2 fusion.12
  124.8 0.2 fusion.11
  125.0 0.2 fusion.52
  125.2 0.2 fusion.51
  125.4 0.2 fusion.10
  125.9 0.2 fusion.9
  126.1 0.2 fusion.56
  126.2 0.2 fusion.55
  126.4 0.2 fusion.8
  127.0 0.2 fusion.7
  127.1 0.2 fusion.60
  127.3 0.2 fusion.59
  127.5 0.2 fusion.6
  128.0 0.2 fusion.5
  128.2 0.2 fusion.64
  128.4 0.2 fusion.63
  128.6 0.2 fusion.4
  129.1 0.2 fusion.3
  129.3 0.2 fusion.68
  129.5 0.2 fusion.67
  129.7 0.2 fusion.2
  129.9 0.2 convolution_divide_fusion
  130.2 0.2 convolution_bitcast_fusion
  130.5 0.6 convolution_convert_fusion
  131.1 0.4 all_to_all.45
  131.5 24.0 %all_to_all.53 = bf16[4,20,8192]{2,1,0:T(8,128)(2,1)S(1)} all-to-all(bf16[4,20,8192]{2,1,0:T(8,128)(2,1)S(1)} %all_to_all.45), channel_id=1, replica_groups=mesh['state'=32,'mem'=4] {'mem'}, dimensions={0} | all-to-all | bytes 2621440 | tf_op jit(solution)/shard_map/all_to_all | solution.py:101
  155.5 1.0 copy.75
  156.6 0.7 pad.6
  157.3 2.0 %copy.81 = bf16[3,8,4,8192]{3,1,2,0:T(8,128)(2,1)} copy(bf16[3,8,4,8192]{3,2,1,0:T(4,128)(2,1)S(1)} %bitcast.113) | data formatting | bytes 3145728
  (40 shorter events, 3.6 us)
Async XLA Ops:
  6.7 17.5 %copy-start = (bf16[20,32768]{1,0:T(8,128)(2,1)S(1)}, bf16[20,32768]{1,0:T(8,128)(2,1)}, u32[]{:S(2)}) copy-start(bf16[20,32768]{1,0:T(8,128)(2,1)} %param.5) | copy-start | bytes 3932164
  24.6 1.1 copy-start.2
  38.2 9.9 %copy-start.1 = (bf16[20,32768]{1,0:T(8,128)(2,1)S(1)}, bf16[20,32768]{1,0:T(8,128)(2,1)}, u32[]{:S(2)}) copy-start(bf16[20,32768]{1,0:T(8,128)(2,1)} %param.5) | copy-start | bytes 3932164
  39.5 18.9 %all-to-all-start = ((f32[32,96,21]{1,2,0:T(8,128)}), f32[32,96,21]{1,2,0:T(8,128)S(1)}, u32[]{:S(2)}, u32[]{:S(2)}) async-start(f32[32,96,21]{1,2,0:T(8,128)} %pad_maximum_fusion), calls=%async_computation | async-start | bytes 786432 | tf_op jit(solution)/shard_map/all_to_all | solution.py:16
  58.3 38.0 %all-to-all-start.2 = ((bf16[20,4,8192]{2,0,1:T(8,128)(2,1)}), bf16[20,4,8192]{2,0,1:T(8,128)(2,1)S(1)}, u32[]{:S(2)}, u32[]{:S(2)}) async-start(bf16[20,4,8192]{2,0,1:T(8,128)(2,1)} %copy.74), calls=%async_computation.2 | async-start | bytes 3145728 | tf_op jit(solution)/shard_map/all_to_all | solution.py:97
  97.7 22.0 %all-to-all-start.1 = ((f32[32,1,6480]{2,1,0:T(1,128)}), f32[32,1,6480]{2,1,0:T(1,128)}, u32[]{:S(2)}, u32[]{:S(2)}) async-start(f32[32,1,6480]{2,1,0:T(1,128)} %broadcast_in_dim.8), calls=%async_computation.1 | async-start | bytes 1671168 | tf_op jit(solution)/shard_map/all_to_all | solution.py:23
where the time goes:
time: 160 us; the launch traced here: 159 us
  local copies, waits for them, and re-layouts  43.1 us (27%)
  blocking collectives  34.9 us (22%)
  other arithmetic  27.3 us (17%)
  starting transfers between devices  20.7 us (13%)
  waiting for transfers between devices  20 us (12%)
  matrix products  11.9 us (7%)
    all_to_all x1, blocking collectives, per_device(): lax.all_to_all(updated, 'mem', split_axis=0, concat_axis=1, tiled=True)  24 us
    scatter-add x1, other arithmetic, per_device(): jax.ops.segment_sum(arrived, arrived_place.astype(jnp.int32), num_segment...  17.5 us
    gather x2, local copies, waits for them, and re-layouts, per_device(): local_place = (slot_ids[order] % share_width).astype(jnp.float32)  17.5 us
    all_to_all x1, waiting for transfers between devices, copy_for_each(): lax.all_to_all(jnp.broadcast_to(x[None], (peers, *x.shape)), axis, 0, 0,...  14.4 us
    all_gather x1, blocking collectives, gather_members(): lax.all_gather(shares.astype(jnp.bfloat16), 'mem', axis=0, tiled=True)  10.9 us
    all_to_all x1, starting transfers between devices, sent_together(): lax.all_to_all(both, axis, split_axis=split_dim, concat_axis=concat_dim,...  8.58 us
    gather x1, local copies, waits for them, and re-layouts, per_device(): sorted_values = values[order]  8.12 us
    all_to_all x1, starting transfers between devices, copy_for_each(): lax.all_to_all(jnp.broadcast_to(x[None], (peers, *x.shape)), axis, 0, 0,...  7.1 us
  transfers between devices with their start and end apart: 3, of which 2 were waited for; matrix products, arithmetic and copies ran while one was open for 15% of the time, Pallas kernels for 0%

commit v1 on v0

v1 whole, which is shorter than its diff:
```python
import functools
import math

import jax
import jax.numpy as jnp
from jax import lax
from jax.experimental import pallas as pl
from jax.experimental.pallas import tpu as pltpu
from jax.sharding import PartitionSpec as P

ITERS = 14
F32, BF16, I32 = jnp.float32, jnp.bfloat16, jnp.int32
MESH = pl.DeviceIdType.MESH
GT = 16
LANES = 128


def nt(a, b, precision=None):
    return lax.dot_general(
        a, b, (((1,), (1,)), ((), ())), precision=precision, preferred_element_type=F32
    )


def iota(shape, dim):
    return lax.broadcasted_iota(I32, shape, dim)


def onehot(mask):
    return jnp.where(mask, 1.0, 0.0)


def transform(total, members, yref, zref):
    hi = lax.Precision.HIGHEST
    total = jnp.concatenate([total, jnp.zeros((LANES - members, LANES), F32)], axis=0)
    down, across = iota((LANES, LANES), 0), iota((LANES, LANES), 1)
    gram = jnp.where(across < members, total, 0.0)
    identity = onehot(jnp.logical_and(down == across, down < members))
    system = (members - 1.0) * identity + gram
    scaling = jnp.sqrt(jnp.sum(jnp.sum(system * system, axis=1, keepdims=True), axis=0, keepdims=True))
    yref[...] = system / scaling
    zref[...] = identity

    def step(_, carry):
        y, z = yref[...], zref[...]
        c = 1.5 * identity - 0.5 * jnp.dot(z, y, precision=hi, preferred_element_type=F32)
        yref[...] = jnp.dot(y, c, precision=hi, preferred_element_type=F32)
        zref[...] = jnp.dot(c, z, precision=hi, preferred_element_type=F32)
        return carry

    lax.fori_loop(0, ITERS, step, 0)
    root = zref[...] / jnp.sqrt(scaling)
    once = jnp.dot(root, total, precision=hi, preferred_element_type=F32)
    twice = jnp.dot(root, once, precision=hi, preferred_element_type=F32)
    mixed = twice[:, members : members + 1] + math.sqrt(members - 1.0) * root
    mixed = mixed + (1.0 - jnp.sum(mixed, axis=0, keepdims=True)) / members
    return jnp.where(jnp.logical_and(down < members, across < members), mixed, 0.0)


def kernel(
    ns, nm, own, tiles, slots, share, route, nown,
    ens, wts, ids, obs, var,
    g16, g4, mix16, mix4,
    yref, zref, tab, rgt, e16, e4, wv, idv, ob, va, vs, lhs, sel, acc, pk, rx, acc2, hg, hf, an, wa, gr, rbuf, gs,
    lsem, bs, br, ps, pr, zs, zr, s1, r1, s2, r2,
):
    me = lax.axis_index("state")
    z = lax.axis_index("mem")
    groups = tiles // GT
    cells = tiles * LANES
    half = cells // 2
    his = share // LANES
    members = own * nm
    chunk = members // nown
    stride = ns // nown
    col = GT * GT

    loads = [
        pltpu.make_async_copy(ens.at[pl.ds(0, 16)], e16, lsem.at[0]),
        pltpu.make_async_copy(ens.at[pl.ds(16, own - 16)], e4, lsem.at[1]),
        pltpu.make_async_copy(wts, wv, lsem.at[2]),
        pltpu.make_async_copy(ids, idv, lsem.at[3]),
        pltpu.make_async_copy(obs.at[me], ob, lsem.at[4]),
        pltpu.make_async_copy(var.at[me], va, lsem.at[5]),
    ]
    for c in loads:
        c.start()

    def plane(d):
        return {"state": lax.rem(me + d, ns)}

    def along(d):
        return {"mem": lax.rem(z + d, nm)}

    barrier = pltpu.get_barrier_semaphore()
    for d in range(1, nm):
        pl.semaphore_signal(barrier, inc=1, device_id=along(d), device_id_type=MESH)

    def greet(d, carry):
        pl.semaphore_signal(barrier, inc=1, device_id=plane(d), device_id_type=MESH)
        return carry

    lax.fori_loop(1, ns, greet, 0)
    pl.semaphore_wait(barrier, nm - 1 + ns - 1)

    def bulk(src16, src4, slot, part, d, n):
        cut = pl.ds(part * half, half)
        return [
            pltpu.make_async_remote_copy(
                src16.at[:, cut], g16.at[slot, :, cut], bs.at[2 * n], br.at[2 * n],
                device_id=along(d), device_id_type=MESH),
            pltpu.make_async_remote_copy(
                src4.at[:, cut], g4.at[slot, :, cut], bs.at[2 * n + 1], br.at[2 * n + 1],
                device_id=along(d), device_id_type=MESH),
        ]

    up0 = bulk(e16, e4, 0, 0, 1, 0)
    dn1 = bulk(e16, e4, 1, 1, nm - 1, 1)
    up1 = bulk(e16, e4, 0, 1, 1, 2)
    dn0 = bulk(e16, e4, 1, 0, nm - 1, 3)
    fu = bulk(g16.at[0], g4.at[0], 2, 0, 1, 4)
    fd = bulk(g16.at[1], g4.at[1], 2, 1, nm - 1, 5)
    loads[0].wait()
    loads[1].wait()
    for c in up0 + dn1:
        c.start()

    loads[3].wait()
    raw = jnp.concatenate([idv[...], jnp.zeros((GT - slots, tiles), I32)], axis=0)
    tab[:tiles] = onehot(iota((tiles, col), 0) % GT == iota((tiles, col), 1) % GT).astype(BF16)
    spread = tab[:tiles]

    def regroup(part):
        part = part.astype(F32)
        tall = jnp.concatenate(
            [jnp.where(iota((GT, tiles), 1) // GT == g, part, 0.0) for g in range(groups)], axis=0
        ).astype(BF16)
        out = jnp.dot(tall, spread, preferred_element_type=F32).reshape(groups, GT, col)
        keep = iota((groups, GT, col), 1) == iota((groups, GT, col), 2) // GT
        return jnp.sum(jnp.where(keep, out, 0.0), axis=1)

    ident = (regroup(raw // 256) * 256.0 + regroup(raw % 256)).astype(I32)
    ident = jnp.where(iota((groups, col), 1) < slots * GT, ident, -1)
    owner = ident // share
    owner = jnp.where(ident < 0, -1, owner)
    place = ident % share
    p_hi = (place // LANES).astype(F32)
    p_lo = (place % LANES).astype(F32)

    ones = [onehot(iota((ns, col), 0) == owner[g : g + 1]) for g in range(groups)]
    tab[...] = onehot(iota((col, col), 0) < iota((col, col), 1)).astype(BF16)
    upper = tab[...]
    before = jnp.dot(
        jnp.concatenate([a.astype(BF16) for a in ones], axis=0), upper, preferred_element_type=F32
    )
    run = jnp.zeros((ns, 1), F32)
    for g in range(groups):
        rank = jnp.sum(ones[g] * (before[g * ns : (g + 1) * ns] + run), axis=0, keepdims=True)
        run = run + jnp.sum(ones[g], axis=1, keepdims=True)
        sel[:, g * col : (g + 1) * col] = onehot(
            iota((LANES, col), 0) == rank.astype(I32)
        ).astype(BF16)

    loads[2].wait()
    lane = iota((GT, col), 1) % GT
    row = iota((GT, col), 0)
    for g in range(groups):
        w = jnp.concatenate(
            [wv[:, g].reshape(slots * GT, LANES), jnp.zeros((col - slots * GT, LANES), BF16)], axis=0
        )
        a = e16[:, g * GT * LANES : (g + 1) * GT * LANES]
        b = e4[:, g * GT * LANES : (g + 1) * GT * LANES]
        b = jnp.concatenate([b, jnp.zeros((32 - own, GT * LANES), BF16)], axis=0)
        va16 = nt(jnp.concatenate([a[:, t * LANES : (t + 1) * LANES] for t in range(GT)], axis=0), w)
        va4 = nt(jnp.concatenate([b[:, t * LANES : (t + 1) * LANES] for t in range(GT)], axis=0), w)
        first = jnp.zeros((GT, col), F32)
        second = jnp.zeros((GT, col), F32)
        for t in range(GT):
            first = jnp.where(lane == t, va16[t * GT : (t + 1) * GT], first)
            second = jnp.where(lane == t, va4[t * GT : (t + 1) * GT], second)
        second = jnp.where(row == own - 16, p_hi[g : g + 1], second)
        second = jnp.where(row == own - 15, p_lo[g : g + 1], second)
        both = jnp.concatenate([first, second], axis=0)
        for o in range(ns):
            lhs[o * 32 : (o + 1) * 32, :] = jnp.where(owner[g : g + 1] == o, both, 0.0).astype(BF16)
        part = nt(lhs[...], sel[:, g * col : (g + 1) * col])
        if g == 0:
            acc[...] = part
        else:
            acc[...] += part
    for o in range(ns):
        pk[o] = acc[o * 32 : (o + 1) * 32, :].astype(BF16)

    def packet(d):
        return pltpu.make_async_remote_copy(
            pk.at[lax.rem(me + d, ns)], rx.at[me], ps.at[d], pr.at[d],
            device_id=plane(d), device_id_type=MESH)

    def arrival(d):
        return pltpu.make_async_remote_copy(
            pk.at[lax.rem(me + d, ns)], rx.at[lax.rem(me - d + ns, ns)], ps.at[d], pr.at[d],
            device_id=plane(d), device_id_type=MESH)

    def send(d, carry):
        packet(d).start()
        return carry

    def receive(d, carry):
        arrival(d).wait_recv()
        return carry

    lax.fori_loop(1, ns, send, 0)
    rx[me] = pk[me]
    lax.fori_loop(1, ns, receive, 0)

    def gather(i, carry):
        left = []
        for q in range(4):
            p = rx[i * 4 + q].astype(F32)
            top = iota((his, LANES), 0).astype(F32) == p[own : own + 1]
            left.append(
                jnp.concatenate([jnp.where(top, p[k : k + 1], 0.0) for k in range(own)], axis=0).astype(BF16)
            )
            rgt[:, q * LANES : (q + 1) * LANES] = onehot(
                iota((LANES, LANES), 0).astype(F32) == p[own + 1 : own + 2]
            ).astype(BF16)
        acc2[...] += nt(jnp.concatenate(left, axis=1), rgt[...])
        return carry

    acc2[...] = jnp.zeros_like(acc2)
    lax.fori_loop(0, ns // 4, gather, 0)
    hg[z] = acc2[...].astype(BF16)

    def members_copy(d, slot):
        return pltpu.make_async_remote_copy(
            hg.at[z], hg.at[slot], zs.at[d - 1], zr.at[d - 1], device_id=along(d), device_id_type=MESH)

    for d in range(1, nm):
        members_copy(d, z).start()
    for c in up0 + dn1:
        c.wait_recv()
    for c in up1 + dn0 + fu + fd:
        c.start()
    for d in range(1, nm):
        members_copy(d, lax.rem(z - d + nm, nm)).wait_recv()

    loads[4].wait()
    loads[5].wait()
    hf[...] = hg[...].astype(F32).reshape(members * his, LANES)
    for h in range(his):
        x = hf[pl.ds(h, members, stride=his), :]
        ybar = jnp.sum(x, axis=0, keepdims=True) / members
        dev = x - ybar
        an[:members, h * LANES : (h + 1) * LANES] = dev
        an[members:, h * LANES : (h + 1) * LANES] = jnp.where(
            iota((LANES - members, LANES), 0) == 0, ob[h : h + 1] - ybar, 0.0
        )
        wa[:, h * LANES : (h + 1) * LANES] = dev * va[h : h + 1]
    gr[...] = nt(wa[...], an[...], lax.Precision.HIGHEST).reshape(nown, chunk, LANES)

    mine = me // stride
    owns = jnp.logical_and(lax.rem(me, stride) == 0, mine < nown)

    def to_owner(i):
        return pltpu.make_async_remote_copy(
            gr.at[i], rbuf.at[me], s1.at[i], r1.at[me],
            device_id={"state": i * stride}, device_id_type=MESH)

    def from_peer(d):
        src = lax.rem(me + d, ns)
        return pltpu.make_async_remote_copy(
            gr.at[0], rbuf.at[src], s1.at[0], r1.at[src], device_id=plane(d), device_id_type=MESH)

    def spread_copy(d, i):
        return pltpu.make_async_remote_copy(
            gs.at[i], gs.at[i], s2.at[d], r2.at[i], device_id=plane(d), device_id_type=MESH)

    for i in range(nown):
        @pl.when(me != i * stride)
        def _():
            to_owner(i).start()

    @pl.when(owns)
    def _():
        rbuf[me] = gr[mine]

        def wait_one(d, carry):
            from_peer(d).wait_recv()
            return carry

        lax.fori_loop(1, ns, wait_one, 0)
        gs[mine] = jnp.sum(rbuf[...], axis=0)

        def send_one(d, carry):
            spread_copy(d, mine).start()
            return carry

        lax.fori_loop(1, ns, send_one, 0)

    for i in range(nown):
        @pl.when(me != i * stride)
        def _():
            spread_copy(1, i).wait_recv()

    mixing = transform(gs[...].reshape(members, LANES), members, yref, zref).astype(BF16)

    rows = 32
    pick = onehot(
        jnp.logical_and(
            iota((rows, LANES), 1) == z * own + iota((rows, LANES), 0), iota((rows, LANES), 0) < own
        )
    ).astype(BF16)
    mine_t = nt(pick, mixing).astype(BF16)
    order = [0, nm - 1, 1, 2]
    for r, d in enumerate(order):
        base = lax.rem(z + d, nm) * own
        tab[:LANES, :LANES] = onehot(iota((LANES, LANES), 0) == base + iota((LANES, LANES), 1)).astype(BF16)
        part = jnp.dot(mine_t, tab[:LANES, :LANES], preferred_element_type=F32)
        mix16[r] = part[:own, :16].astype(BF16)
        mix4[r] = part[:own, 16:own].astype(BF16)

    for c in up0 + dn1:
        c.wait_send()
    for c in up1 + dn0 + fu + fd:
        c.wait()

    def drain(d, carry):
        packet(d).wait_send()
        return carry

    lax.fori_loop(1, ns, drain, 0)
    for d in range(1, nm):
        members_copy(d, z).wait_send()
    for i in range(nown):
        @pl.when(me != i * stride)
        def _():
            to_owner(i).wait_send()

    @pl.when(owns)
    def _():
        def drain2(d, carry):
            spread_copy(d, mine).wait_send()
            return carry

        lax.fori_loop(1, ns, drain2, 0)


def final(own, ens, g16, g4, mix16, mix4, out):
    x = ens[...]
    total = jnp.dot(mix16[0], x[:16], preferred_element_type=F32)
    total += jnp.dot(mix4[0], x[16:], preferred_element_type=F32)
    for r in range(3):
        total += jnp.dot(mix16[r + 1], g16[r], preferred_element_type=F32)
        total += jnp.dot(mix4[r + 1], g4[r], preferred_element_type=F32)
    out[...] = total.astype(BF16)


def per_device(ns, nm, ensemble, weights, seg_obs, observed, inv_var):
    own, cells = ensemble.shape
    tiles, slots, _ = weights.shape
    share = observed.shape[0] // ns
    route = tiles * slots // ns
    members = own * nm
    nown = 10 if ns >= 10 else 2
    groups = tiles // GT
    his = share // LANES
    wts = jnp.transpose(weights, (1, 0, 2)).reshape(slots, groups, GT, LANES)
    ids = jnp.transpose(seg_obs)
    obs = observed.reshape(ns, his, LANES)
    var = inv_var.reshape(ns, his, LANES)
    anyspec = pl.BlockSpec(memory_space=pl.ANY)
    vspec = pl.BlockSpec(memory_space=pltpu.VMEM)
    dma = pltpu.SemaphoreType.DMA
    col = GT * GT
    g16, g4, mix16, mix4 = pl.pallas_call(
        functools.partial(kernel, ns, nm, own, tiles, slots, share, route, nown),
        out_shape=(
            jax.ShapeDtypeStruct((3, 16, cells), BF16),
            jax.ShapeDtypeStruct((3, own - 16, cells), BF16),
            jax.ShapeDtypeStruct((nm, own, 16), BF16),
            jax.ShapeDtypeStruct((nm, own, own - 16), BF16),
        ),
        in_specs=[anyspec] * 5,
        out_specs=(anyspec, anyspec, vspec, vspec),
        scratch_shapes=[
            pltpu.VMEM((LANES, LANES), F32),
            pltpu.VMEM((LANES, LANES), F32),
            pltpu.VMEM((col, col), BF16),
            pltpu.VMEM((LANES, 4 * LANES), BF16),
            pltpu.VMEM((16, cells), BF16),
            pltpu.VMEM((own - 16, cells), BF16),
            pltpu.VMEM((slots, groups, GT, LANES), BF16),
            pltpu.VMEM((slots, tiles), I32),
            pltpu.VMEM((his, LANES), F32),
            pltpu.VMEM((his, LANES), F32),
            pltpu.VMEM((32, groups * col), BF16),
            pltpu.VMEM((ns * 32, col), BF16),
            pltpu.VMEM((LANES, groups * col), BF16),
            pltpu.VMEM((ns * 32, LANES), F32),
            pltpu.VMEM((ns, 32, LANES), BF16),
            pltpu.VMEM((ns, 32, LANES), BF16),
            pltpu.VMEM((own * his, LANES), F32),
            pltpu.VMEM((nm, own * his, LANES), BF16),
            pltpu.VMEM((members * his, LANES), F32),
            pltpu.VMEM((LANES, share), F32),
            pltpu.VMEM((members, share), F32),
            pltpu.VMEM((nown, members // nown, LANES), F32),
            pltpu.VMEM((ns, members // nown, LANES), F32),
            pltpu.VMEM((nown, members // nown, LANES), F32),
            dma((6,)), dma((12,)), dma((12,)), dma((ns,)), dma((ns,)),
            dma((nm - 1,)), dma((nm - 1,)), dma((nown,)), dma((ns,)), dma((ns,)), dma((nown,)),
        ],
        compiler_params=pltpu.CompilerParams(collective_id=0, has_side_effects=True),
        name="assimilate",
    )(ensemble, wts, ids, obs, var)
    step = min(4096, cells)
    return pl.pallas_call(
        functools.partial(final, own),
        out_shape=jax.ShapeDtypeStruct((own, cells), BF16),
        grid=(cells // step,),
        in_specs=[
            pl.BlockSpec((own, step), lambda i: (0, i)),
            pl.BlockSpec((3, 16, step), lambda i: (0, 0, i)),
            pl.BlockSpec((3, own - 16, step), lambda i: (0, 0, i)),
            pl.BlockSpec((nm, own, 16), lambda i: (0, 0, 0)),
            pl.BlockSpec((nm, own, own - 16), lambda i: (0, 0, 0)),
        ],
        out_specs=pl.BlockSpec((own, step), lambda i: (0, i)),
        name="update",
    )(ensemble, g16, g4, mix16, mix4)


def solution(mesh):
    return jax.shard_map(
        functools.partial(per_device, mesh.shape["state"], mesh.shape["mem"]),
        mesh=mesh,
        in_specs=(P("mem", "state"), P("state", None, None), P("state", None), P(), P()),
        out_specs=P("mem", "state"),
        check_vma=False,
    )
```

time: 160 us -> 68.6 us (0.43)
  Pallas kernels: 0 us -> 68.3 us
  local copies, waits for them, and re-layouts: 43.1 us -> 0 us
  blocking collectives: 34.9 us -> 0 us
  other arithmetic: 27.3 us -> 0 us
  starting transfers between devices: 20.7 us -> 0 us
  waiting for transfers between devices: 20 us -> 0 us
  matrix products: 11.9 us -> 0 us
    pallas_call x0 -> x2, Pallas kernels: none -> 68.3 us  [the longest x1 59.5 us: per_device(): pl.pallas_call(functools.partial(kernel, ns, nm, own, tiles, slots, share...]
    gather x3 -> x0, local copies, waits for them, and re-layouts: 25.6 us -> none  [the longest x2 17.5 us: per_device(): local_place = (slot_ids[order] % share_width).astype(jnp.float32)]
    all_to_all x1 -> x0, blocking collectives: 24 us -> none  [per_device(): lax.all_to_all(updated, 'mem', split_axis=0, concat_axis=1, tiled=True)]
    all_to_all x3 -> x0, starting transfers between devices: 20.7 us -> none  [the longest x1 8.58 us: sent_together(): lax.all_to_all(both, axis, split_axis=split_dim, concat_axis=concat_dim,...]
    all_to_all x3 -> x0, waiting for transfers between devices: 20 us -> none  [the longest x1 14.4 us: copy_for_each(): lax.all_to_all(jnp.broadcast_to(x[None], (peers, *x.shape)), axis, 0, 0,...]
    scatter-add x1 -> x0, other arithmetic: 17.5 us -> none  [per_device(): jax.ops.segment_sum(arrived, arrived_place.astype(jnp.int32), num_segment...]
    dot_general x47 -> x0, matrix products: 11.9 us -> none  [the longest x1 2.68 us: per_device(): jnp.einsum('ktc,tjc->tjk', blocks, weights, preferred_element_type=jnp.fl...]
    all_gather x1 -> x0, blocking collectives: 10.9 us -> none  [gather_members(): lax.all_gather(shares.astype(jnp.bfloat16), 'mem', axis=0, tiled=True)]
  transfers between devices with their start and end apart: 3 -> 0, of which waited for: 2 -> 0; matrix products, arithmetic and copies ran while one was open for 15% -> 0% of each run, Pallas kernels for 0% -> 0%
where the time goes in v1:
time: 68.6 us; the launch traced here: 68.3 us
  Pallas kernels  68.3 us (100%)
    pallas_call x1, Pallas kernels, per_device(): pl.pallas_call(functools.partial(kernel, ns, nm, own, tiles, slots, share...  59.5 us
    pallas_call x1, Pallas kernels, per_device(): pl.pallas_call(functools.partial(final, own), out_shape=jax.ShapeDtypeStr...  8.83 us

profile of v1, /device:TPU:1, one launch (start us, length us, event | category | flops | bytes accessed | tf_op | source)
XLA Modules:
  0.0 68.3 jit_solution(568585512399147743)
XLA Ops:
  0.0 59.5 %assimilate.1 = (bf16[3,16,32768]{2,1,0:T(8,128)(2,1)}, bf16[3,4,32768]{2,1,0:T(4,128)(2,1)}, bf16[4,20,16]{2,1,0:T(8,128)(2,1)}, bf16[4,20,4]{2,1,0:T(8,128)(2,1)}) custom-call(bf16[20,32768]{1,0:T(8,128)(2,1)} %ens.3, bf16[12,16,16,128]{3,2,1,0:T(8,128)(2,1)} %bitcast.6, s32[12,256]{1,0:T(8,128)} %bitcast.9, f32[32,16,128]{2,1,0:T(8,128)} %bitcast.7, ...), custom_call_target="tpu_custom_call" | custom-call | tf_op jit(solution)/shard_map/assimilate/pallas_call | solution.py:374
  59.5 8.8 %update.1 = bf16[20,32768]{1,0:T(8,128)(2,1)} custom-call(bf16[20,32768]{1,0:T(8,128)(2,1)} %ens.3, bf16[3,16,32768]{2,1,0:T(8,128)(2,1)} %get-tuple-element.9.g16, bf16[3,4,32768]{2,1,0:T(4,128)(2,1)} %get-tuple-element.10.g4, bf16[4,20,16]{2,1,0:T(8,128)(2,1)} %get-tuple-element.11.mix16, bf16[4,20,4]{2,1,0:T(8,128)(2,1)} %get-tuple-element.12.mix4), custom_call_target="tpu_custom_call" | custom-call | tf_op jit(solution)/shard_map/update/pallas_call | solution.py:416

commit v2 on v1

--- a/solution.py
+++ b/solution.py
@@ -12,6 +12,7 @@
 F32, BF16, I32 = jnp.float32, jnp.bfloat16, jnp.int32
 MESH = pl.DeviceIdType.MESH
 GT = 16
+START = 10
 LANES = 128
 
 
@@ -29,38 +30,56 @@
     return jnp.where(mask, 1.0, 0.0)
 
 
+def split(x):
+    high = x.astype(BF16)
+    return high, (x - high.astype(F32)).astype(BF16)
+
+
+def tall(x):
+    high, low = split(x)
+    pad = jnp.zeros((LANES - x.shape[0], LANES), BF16)
+    return jnp.concatenate([high, pad, high, pad, low, pad], axis=0)
+
+
+def wide(x):
+    high, low = split(x)
+    return jnp.concatenate([high, low, high], axis=1)
+
+
+def product(left, right):
+    return jnp.dot(left, right, preferred_element_type=F32)
+
+
 def transform(total, members, yref, zref):
-    hi = lax.Precision.HIGHEST
-    total = jnp.concatenate([total, jnp.zeros((LANES - members, LANES), F32)], axis=0)
-    down, across = iota((LANES, LANES), 0), iota((LANES, LANES), 1)
-    gram = jnp.where(across < members, total, 0.0)
-    identity = onehot(jnp.logical_and(down == across, down < members))
-    system = (members - 1.0) * identity + gram
+    shape = (members, LANES)
+    down, across = iota(shape, 0), iota(shape, 1)
+    identity = onehot(down == across)
+    system = (members - 1.0) * identity + jnp.where(across < members, total, 0.0)
     scaling = jnp.sqrt(jnp.sum(jnp.sum(system * system, axis=1, keepdims=True), axis=0, keepdims=True))
     yref[...] = system / scaling
     zref[...] = identity
 
     def step(_, carry):
         y, z = yref[...], zref[...]
-        c = 1.5 * identity - 0.5 * jnp.dot(z, y, precision=hi, preferred_element_type=F32)
-        yref[...] = jnp.dot(y, c, precision=hi, preferred_element_type=F32)
-        zref[...] = jnp.dot(c, z, precision=hi, preferred_element_type=F32)
+        c = 1.5 * identity - 0.5 * product(wide(z), tall(y))
+        yref[...] = product(wide(y), tall(c))
+        zref[...] = product(wide(c), tall(z))
         return carry
 
     lax.fori_loop(0, ITERS, step, 0)
     root = zref[...] / jnp.sqrt(scaling)
-    once = jnp.dot(root, total, precision=hi, preferred_element_type=F32)
-    twice = jnp.dot(root, once, precision=hi, preferred_element_type=F32)
+    left = wide(root)
+    twice = product(left, tall(product(left, tall(total))))
     mixed = twice[:, members : members + 1] + math.sqrt(members - 1.0) * root
     mixed = mixed + (1.0 - jnp.sum(mixed, axis=0, keepdims=True)) / members
-    return jnp.where(jnp.logical_and(down < members, across < members), mixed, 0.0)
+    return jnp.where(across < members, mixed, 0.0)
 
 
 def kernel(
     ns, nm, own, tiles, slots, share, route, nown,
     ens, wts, ids, obs, var,
-    g16, g4, mix16, mix4,
-    yref, zref, tab, rgt, e16, e4, wv, idv, ob, va, vs, lhs, sel, acc, pk, rx, acc2, hg, hf, an, wa, gr, rbuf, gs,
+    g16, g4, mix,
+    yref, zref, tab, rgt, e16, e4, wv, idv, ob, va, lhs, sel, acc, pk, rx, acc2, hg, hf, an, wa, gr, rbuf, gs,
     lsem, bs, br, ps, pr, zs, zr, s1, r1, s2, r2,
 ):
     me = lax.axis_index("state")
@@ -100,7 +119,6 @@
         return carry
 
     lax.fori_loop(1, ns, greet, 0)
-    pl.semaphore_wait(barrier, nm - 1 + ns - 1)
 
     def bulk(src16, src4, slot, part, d, n):
         cut = pl.ds(part * half, half)
@@ -119,10 +137,6 @@
     dn0 = bulk(e16, e4, 1, 0, nm - 1, 3)
     fu = bulk(g16.at[0], g4.at[0], 2, 0, 1, 4)
     fd = bulk(g16.at[1], g4.at[1], 2, 1, nm - 1, 5)
-    loads[0].wait()
-    loads[1].wait()
-    for c in up0 + dn1:
-        c.start()
 
     loads[3].wait()
     raw = jnp.concatenate([idv[...], jnp.zeros((GT - slots, tiles), I32)], axis=0)
@@ -143,8 +157,7 @@
     owner = ident // share
     owner = jnp.where(ident < 0, -1, owner)
     place = ident % share
-    p_hi = (place // LANES).astype(F32)
-    p_lo = (place % LANES).astype(F32)
+    code = jnp.left_shift(1, place // LANES).astype(F32) * (1.0 + (place % LANES).astype(F32) / LANES)
 
     ones = [onehot(iota((ns, col), 0) == owner[g : g + 1]) for g in range(groups)]
     tab[...] = onehot(iota((col, col), 0) < iota((col, col), 1)).astype(BF16)
@@ -153,14 +166,20 @@
         jnp.concatenate([a.astype(BF16) for a in ones], axis=0), upper, preferred_element_type=F32
     )
     run = jnp.zeros((ns, 1), F32)
+    ranks = []
     for g in range(groups):
         rank = jnp.sum(ones[g] * (before[g * ns : (g + 1) * ns] + run), axis=0, keepdims=True)
         run = run + jnp.sum(ones[g], axis=1, keepdims=True)
-        sel[:, g * col : (g + 1) * col] = onehot(
-            iota((LANES, col), 0) == rank.astype(I32)
+        rank = rank.astype(I32)
+        ranks.append(rank)
+        sel[:, 2 * g * col : (2 * g + 1) * col] = onehot(iota((LANES, col), 0) == rank).astype(BF16)
+        sel[:, (2 * g + 1) * col : (2 * g + 2) * col] = onehot(
+            iota((LANES, col), 0) == LANES - 32 + rank % 32
         ).astype(BF16)
 
     loads[2].wait()
+    loads[0].wait()
+    loads[1].wait()
     lane = iota((GT, col), 1) % GT
     row = iota((GT, col), 0)
     for g in range(groups):
@@ -177,18 +196,26 @@
         for t in range(GT):
             first = jnp.where(lane == t, va16[t * GT : (t + 1) * GT], first)
             second = jnp.where(lane == t, va4[t * GT : (t + 1) * GT], second)
-        second = jnp.where(row == own - 16, p_hi[g : g + 1], second)
-        second = jnp.where(row == own - 15, p_lo[g : g + 1], second)
-        both = jnp.concatenate([first, second], axis=0)
+        extra = [second[r : r + 1] for r in range(own - 16)] + [code[g : g + 1]]
+        rest = jnp.zeros((GT, col), F32)
+        for r, line in enumerate(extra):
+            rest = jnp.where(row // 3 == r, line, rest)
+        rest = jnp.where(row % 3 == ranks[g] // 32, rest, 0.0)
         for o in range(ns):
-            lhs[o * 32 : (o + 1) * 32, :] = jnp.where(owner[g : g + 1] == o, both, 0.0).astype(BF16)
-        part = nt(lhs[...], sel[:, g * col : (g + 1) * col])
+            there = owner[g : g + 1] == o
+            lhs[o * GT : (o + 1) * GT, :col] = jnp.where(there, first, 0.0).astype(BF16)
+            lhs[o * GT : (o + 1) * GT, col:] = jnp.where(there, rest, 0.0).astype(BF16)
+        part = nt(lhs[...], sel[:, 2 * g * col : (2 * g + 2) * col])
         if g == 0:
             acc[...] = part
         else:
             acc[...] += part
+        if g == min(START, groups) - 1:
+            pl.semaphore_wait(barrier, nm - 1 + ns - 1)
+            for c in up0 + dn1:
+                c.start()
     for o in range(ns):
-        pk[o] = acc[o * 32 : (o + 1) * 32, :].astype(BF16)
+        pk[o] = acc[o * GT : (o + 1) * GT, :].astype(BF16)
 
     def packet(d):
         return pltpu.make_async_remote_copy(
@@ -211,18 +238,28 @@
     lax.fori_loop(1, ns, send, 0)
     rx[me] = pk[me]
     lax.fori_loop(1, ns, receive, 0)
+
+    spot = iota((1, LANES), 1)
+    power = jnp.left_shift(1, iota((his, LANES), 0)).astype(F32)
+    inverse = jnp.left_shift(1, his - 1 - iota((his, LANES), 0)).astype(F32) * (2.0 ** (1 - his))
 
     def gather(i, carry):
         left = []
         for q in range(4):
             p = rx[i * 4 + q].astype(F32)
-            top = iota((his, LANES), 0).astype(F32) == p[own : own + 1]
+            r1x, r2x, r3x = (pltpu.roll(p, 32 * (t + 1), 1) for t in range(3))
+            lines = [p[k : k + 1] for k in range(16)]
+            for r in range(own - 15):
+                line = jnp.where(spot < 96, r3x[3 * r + 2 : 3 * r + 3], 0.0)
+                line = jnp.where(spot < 64, r2x[3 * r + 1 : 3 * r + 2], line)
+                lines.append(jnp.where(spot < 32, r1x[3 * r : 3 * r + 1], line))
+            where = lines.pop()
+            top = jnp.logical_and(where >= power, where < 2.0 * power)
             left.append(
-                jnp.concatenate([jnp.where(top, p[k : k + 1], 0.0) for k in range(own)], axis=0).astype(BF16)
+                jnp.concatenate([jnp.where(top, v, 0.0) for v in lines], axis=0).astype(BF16)
             )
-            rgt[:, q * LANES : (q + 1) * LANES] = onehot(
-                iota((LANES, LANES), 0).astype(F32) == p[own + 1 : own + 2]
-            ).astype(BF16)
+            low = where * jnp.sum(jnp.where(top, inverse, 0.0), axis=0, keepdims=True) * LANES - LANES
+            rgt[:, q * LANES : (q + 1) * LANES] = onehot(iota((LANES, LANES), 0).astype(F32) == low).astype(BF16)
         acc2[...] += nt(jnp.concatenate(left, axis=1), rgt[...])
         return carry
 
@@ -304,19 +341,16 @@
     mixing = transform(gs[...].reshape(members, LANES), members, yref, zref).astype(BF16)
 
     rows = 32
-    pick = onehot(
-        jnp.logical_and(
-            iota((rows, LANES), 1) == z * own + iota((rows, LANES), 0), iota((rows, LANES), 0) < own
-        )
-    ).astype(BF16)
-    mine_t = nt(pick, mixing).astype(BF16)
-    order = [0, nm - 1, 1, 2]
-    for r, d in enumerate(order):
-        base = lax.rem(z + d, nm) * own
-        tab[:LANES, :LANES] = onehot(iota((LANES, LANES), 0) == base + iota((LANES, LANES), 1)).astype(BF16)
-        part = jnp.dot(mine_t, tab[:LANES, :LANES], preferred_element_type=F32)
-        mix16[r] = part[:own, :16].astype(BF16)
-        mix4[r] = part[:own, 16:own].astype(BF16)
+    k = iota((rows, LANES), 0)
+    pick = onehot(jnp.logical_and(iota((rows, LANES), 1) == z * own + k, k < own)).astype(BF16)
+    q = iota((members, LANES), 0)
+    slot = jnp.where(q < 16 * nm, q // 16, (q - 16 * nm) // (own - 16))
+    inner = jnp.where(q < 16 * nm, q % 16, 16 + (q - 16 * nm) % (own - 16))
+    dist = jnp.where(slot == 0, 0, jnp.where(slot == 1, nm - 1, slot - 1))
+    tab[:members, :LANES] = onehot(iota((members, LANES), 1) == (z + dist) % nm * own + inner).astype(BF16)
+    padded = jnp.concatenate([mixing, jnp.zeros((LANES - members, LANES), BF16)], axis=0)
+    mine_t = nt(pick, padded).astype(BF16)
+    mix[...] = nt(mine_t, tab[:members, :LANES]).astype(BF16)
 
     for c in up0 + dn1:
         c.wait_send()
@@ -344,14 +378,12 @@
         lax.fori_loop(1, ns, drain2, 0)
 
 
-def final(own, ens, g16, g4, mix16, mix4, out):
+def final(own, ens, g16, g4, mix, out):
     x = ens[...]
-    total = jnp.dot(mix16[0], x[:16], preferred_element_type=F32)
-    total += jnp.dot(mix4[0], x[16:], preferred_element_type=F32)
-    for r in range(3):
-        total += jnp.dot(mix16[r + 1], g16[r], preferred_element_type=F32)
-        total += jnp.dot(mix4[r + 1], g4[r], preferred_element_type=F32)
-    out[...] = total.astype(BF16)
+    parts = [x[:16]] + [g16[r] for r in range(3)]
+    parts.append(jnp.concatenate([x[16:]] + [g4[r] for r in range(3)], axis=0))
+    total = jnp.dot(mix[...], jnp.concatenate(parts, axis=0), preferred_element_type=F32)
+    out[...] = total[:own].astype(BF16)
 
 
 def per_device(ns, nm, ensemble, weights, seg_obs, observed, inv_var):
@@ -371,19 +403,18 @@
     vspec = pl.BlockSpec(memory_space=pltpu.VMEM)
     dma = pltpu.SemaphoreType.DMA
     col = GT * GT
-    g16, g4, mix16, mix4 = pl.pallas_call(
+    g16, g4, mix = pl.pallas_call(
         functools.partial(kernel, ns, nm, own, tiles, slots, share, route, nown),
         out_shape=(
             jax.ShapeDtypeStruct((3, 16, cells), BF16),
             jax.ShapeDtypeStruct((3, own - 16, cells), BF16),
-            jax.ShapeDtypeStruct((nm, own, 16), BF16),
-            jax.ShapeDtypeStruct((nm, own, own - 16), BF16),
+            jax.ShapeDtypeStruct((32, members), BF16),
         ),
         in_specs=[anyspec] * 5,
-        out_specs=(anyspec, anyspec, vspec, vspec),
+        out_specs=(anyspec, anyspec, vspec),
         scratch_shapes=[
-            pltpu.VMEM((LANES, LANES), F32),
-            pltpu.VMEM((LANES, LANES), F32),
+            pltpu.VMEM((members, LANES), F32),
+            pltpu.VMEM((members, LANES), F32),
             pltpu.VMEM((col, col), BF16),
             pltpu.VMEM((LANES, 4 * LANES), BF16),
             pltpu.VMEM((16, cells), BF16),
@@ -392,12 +423,11 @@
             pltpu.VMEM((slots, tiles), I32),
             pltpu.VMEM((his, LANES), F32),
             pltpu.VMEM((his, LANES), F32),
-            pltpu.VMEM((32, groups * col), BF16),
-            pltpu.VMEM((ns * 32, col), BF16),
-            pltpu.VMEM((LANES, groups * col), BF16),
-            pltpu.VMEM((ns * 32, LANES), F32),
-            pltpu.VMEM((ns, 32, LANES), BF16),
-            pltpu.VMEM((ns, 32, LANES), BF16),
+            pltpu.VMEM((ns * GT, 2 * col), BF16),
+            pltpu.VMEM((LANES, 2 * groups * col), BF16),
+            pltpu.VMEM((ns * GT, LANES), F32),
+            pltpu.VMEM((ns, GT, LANES), BF16),
+            pltpu.VMEM((ns, GT, LANES), BF16),
             pltpu.VMEM((own * his, LANES), F32),
             pltpu.VMEM((nm, own * his, LANES), BF16),
             pltpu.VMEM((members * his, LANES), F32),
@@ -421,12 +451,11 @@
             pl.BlockSpec((own, step), lambda i: (0, i)),
             pl.BlockSpec((3, 16, step), lambda i: (0, 0, i)),
             pl.BlockSpec((3, own - 16, step), lambda i: (0, 0, i)),
-            pl.BlockSpec((nm, own, 16), lambda i: (0, 0, 0)),
-            pl.BlockSpec((nm, own, own - 16), lambda i: (0, 0, 0)),
+            pl.BlockSpec((32, members), lambda i: (0, 0)),
         ],
         out_specs=pl.BlockSpec((own, step), lambda i: (0, i)),
         name="update",
-    )(ensemble, g16, g4, mix16, mix4)
+    )(ensemble, g16, g4, mix)
 
 
 def solution(mesh):

time: 68.6 us -> 66.7 us (0.972)
  Pallas kernels: 68.3 us -> 66.3 us
    pallas_call x1, Pallas kernels: 8.83 us -> 7 us  [per_device(): pl.pallas_call(functools.partial(final, own), out_shape=jax.ShapeDtypeStr...]
where the time goes in v2:
time: 66.7 us; the launch traced here: 66.3 us
  Pallas kernels  66.3 us (99%)
    pallas_call x1, Pallas kernels, per_device(): pl.pallas_call(functools.partial(kernel, ns, nm, own, tiles, slots, share...  59.3 us
    pallas_call x1, Pallas kernels, per_device(): pl.pallas_call(functools.partial(final, own), out_shape=jax.ShapeDtypeStr...  7 us

profile of v2, /device:TPU:1, one launch (start us, length us, event | category | flops | bytes accessed | tf_op | source)
XLA Modules:
  0.0 66.3 jit_solution(2020387466709477045)
XLA Ops:
  0.0 59.3 %assimilate.1 = (bf16[3,16,32768]{2,1,0:T(8,128)(2,1)}, bf16[3,4,32768]{2,1,0:T(4,128)(2,1)}, bf16[32,80]{1,0:T(8,128)(2,1)}) custom-call(bf16[20,32768]{1,0:T(8,128)(2,1)} %ens.3, bf16[12,16,16,128]{3,2,1,0:T(8,128)(2,1)} %bitcast.6, s32[12,256]{1,0:T(8,128)} %bitcast.9, f32[32,16,128]{2,1,0:T(8,128)} %bitcast.7, f32[32,16,128]{2,1,0:T(8,128)} %bitcast.8), custom_call_target="tpu_custom_call" | custom-call | tf_op jit(solution)/shard_map/assimilate/pallas_call | solution.py:406
  59.3 7.0 %update.1 = bf16[20,32768]{1,0:T(8,128)(2,1)} custom-call(bf16[20,32768]{1,0:T(8,128)(2,1)} %ens.3, bf16[3,16,32768]{2,1,0:T(8,128)(2,1)} %get-tuple-element.8.g16, bf16[3,4,32768]{2,1,0:T(4,128)(2,1)} %get-tuple-element.9.g4, bf16[32,80]{1,0:T(8,128)(2,1)} %get-tuple-element.10.mix), custom_call_target="tpu_custom_call" | custom-call | tf_op jit(solution)/shard_map/update/pallas_call | solution.py:446

commit v3 on v2

--- a/solution.py
+++ b/solution.py
@@ -12,6 +12,8 @@
 F32, BF16, I32 = jnp.float32, jnp.bfloat16, jnp.int32
 MESH = pl.DeviceIdType.MESH
 GT = 16
+FULL = 8
+FSTEPS = 4
 START = 10
 LANES = 128
 
@@ -76,17 +78,18 @@
 
 
 def kernel(
-    ns, nm, own, tiles, slots, share, route, nown,
+    ns, nm, own, tiles, slots, share, nown, fc,
     ens, wts, ids, obs, var,
-    g16, g4, mix,
+    o16, o4,
+    f16, f4, q16, q4, t16, t4, x4, w16, w4, v16, v4, u16, u4, mixp,
     yref, zref, tab, rgt, e16, e4, wv, idv, ob, va, lhs, sel, acc, pk, rx, acc2, hg, hf, an, wa, gr, rbuf, gs,
-    lsem, bs, br, ps, pr, zs, zr, s1, r1, s2, r2,
+    lsem, bs, br, ps, pr, zs, zr, s1, r1, s2, r2, osem,
 ):
     me = lax.axis_index("state")
     z = lax.axis_index("mem")
     groups = tiles // GT
     cells = tiles * LANES
-    half = cells // 2
+    qc = (cells - fc) // nm
     his = share // LANES
     members = own * nm
     chunk = members // nown
@@ -120,23 +123,60 @@
 
     lax.fori_loop(1, ns, greet, 0)
 
-    def bulk(src16, src4, slot, part, d, n):
-        cut = pl.ds(part * half, half)
+    count = [0]
+
+    def pair(src16, src4, dst16, dst4, d):
+        n = count[0]
+        count[0] += 2
         return [
             pltpu.make_async_remote_copy(
-                src16.at[:, cut], g16.at[slot, :, cut], bs.at[2 * n], br.at[2 * n],
-                device_id=along(d), device_id_type=MESH),
-            pltpu.make_async_remote_copy(
-                src4.at[:, cut], g4.at[slot, :, cut], bs.at[2 * n + 1], br.at[2 * n + 1],
-                device_id=along(d), device_id_type=MESH),
+                src, dst, bs.at[n + i], br.at[n + i], device_id=along(d), device_id_type=MESH)
+            for i, (src, dst) in enumerate(((src16, dst16), (src4, dst4)))
         ]
 
-    up0 = bulk(e16, e4, 0, 0, 1, 0)
-    dn1 = bulk(e16, e4, 1, 1, nm - 1, 1)
-    up1 = bulk(e16, e4, 0, 1, 1, 2)
-    dn0 = bulk(e16, e4, 1, 0, nm - 1, 3)
-    fu = bulk(g16.at[0], g4.at[0], 2, 0, 1, 4)
-    fd = bulk(g16.at[1], g4.at[1], 2, 1, nm - 1, 5)
+    up, dn = 1, nm - 1
+    fh, qh = fc // 2, qc // 2
+
+    def quarter(d):
+        return pl.multiple_of(fc + lax.rem(z + d, nm) * qc, LANES)
+
+    def own_at(at, n):
+        return e16.at[:, pl.ds(at, n)], e4.at[:, pl.ds(at, n)]
+
+    def at(pairs, slot, start, n):
+        return tuple(ref.at[slot, :, pl.ds(start, n)] for ref in pairs)
+
+    first_up = pair(*own_at(quarter(2), qh), *at((t16, t4), 0, 0, qh), up)
+    first_dn = pair(*own_at(quarter(2) + qh, qh), *at((t16, t4), 1, 0, qh), dn)
+    near_up = pair(*own_at(quarter(up), qc), *at((q16, q4), 0, 0, qc), up)
+    near_dn = pair(*own_at(quarter(dn), qc), *at((q16, q4), 1, 0, qc), dn)
+    pass_up = pair(*at((t16, t4), 0, 0, qh), *at((q16, q4), 2, 0, qh), up)
+    pass_dn = pair(*at((t16, t4), 1, 0, qh), *at((q16, q4), 2, qh, qh), dn)
+    full_up0 = pair(*own_at(0, fh), *at((f16, f4), 0, 0, fh), up)
+    full_dn1 = pair(*own_at(fh, fh), *at((f16, f4), 1, fh, fh), dn)
+    full_up1 = pair(*own_at(fh, fh), *at((f16, f4), 0, fh, fh), up)
+    full_dn0 = pair(*own_at(0, fh), *at((f16, f4), 1, 0, fh), dn)
+    over_up = pair(*at((f16, f4), 0, 0, fh), *at((f16, f4), 2, 0, fh), up)
+    over_dn = pair(*at((f16, f4), 1, fh, fh), *at((f16, f4), 2, fh, fh), dn)
+    wave1 = first_up + first_dn + near_up + near_dn + full_up0 + full_dn1
+    wave2 = pass_up + pass_dn
+    wave3 = full_up1 + full_dn0 + over_up + over_dn
+    mid = pl.multiple_of(fc + z * qc, LANES)
+    far = pl.multiple_of(fc + lax.rem(z + 2, nm) * qc, LANES)
+
+    def out_at(start, n):
+        return o16.at[:, pl.ds(start, n)], o4.at[:, pl.ds(start, n)]
+
+    back_first_up = pair(*at((w16, w4), 3, 0, qh), *at((v16, v4), 0, 0, qh), up)
+    back_first_dn = pair(*at((w16, w4), 3, qh, qh), *at((v16, v4), 1, 0, qh), dn)
+    back_near_up = pair(*at((w16, w4), 2, 0, qc), *out_at(mid, qc), up)
+    back_near_dn = pair(*at((w16, w4), 1, 0, qc), *out_at(mid, qc), dn)
+    before_mid = pl.multiple_of(fc + lax.rem(z + dn, nm) * qc, LANES)
+    after_mid = pl.multiple_of(fc + lax.rem(z + up, nm) * qc, LANES)
+    back_pass_up = pair(*at((v16, v4), 0, 0, qh), *out_at(before_mid, qh), up)
+    back_pass_dn = pair(*at((v16, v4), 1, 0, qh), *out_at(after_mid + qh, qh), dn)
+    back1 = back_first_up + back_first_dn + back_near_up + back_near_dn
+    back2 = back_pass_up + back_pass_dn
 
     loads[3].wait()
     raw = jnp.concatenate([idv[...], jnp.zeros((GT - slots, tiles), I32)], axis=0)
@@ -212,32 +252,27 @@
             acc[...] += part
         if g == min(START, groups) - 1:
             pl.semaphore_wait(barrier, nm - 1 + ns - 1)
-            for c in up0 + dn1:
+            for c in wave1:
                 c.start()
     for o in range(ns):
         pk[o] = acc[o * GT : (o + 1) * GT, :].astype(BF16)
 
-    def packet(d):
-        return pltpu.make_async_remote_copy(
-            pk.at[lax.rem(me + d, ns)], rx.at[me], ps.at[d], pr.at[d],
-            device_id=plane(d), device_id_type=MESH)
-
-    def arrival(d):
-        return pltpu.make_async_remote_copy(
-            pk.at[lax.rem(me + d, ns)], rx.at[lax.rem(me - d + ns, ns)], ps.at[d], pr.at[d],
-            device_id=plane(d), device_id_type=MESH)
-
     def send(d, carry):
-        packet(d).start()
+        pltpu.make_async_remote_copy(
+            pk.at[lax.rem(me + d, ns)], rx.at[me], ps.at[0], pr.at[0],
+            device_id=plane(d), device_id_type=MESH).start()
         return carry
 
-    def receive(d, carry):
-        arrival(d).wait_recv()
-        return carry
-
+    packets = pltpu.make_async_remote_copy(
+        pk.at[pl.ds(0, ns - 1)], rx.at[pl.ds(0, ns - 1)], ps.at[0], pr.at[0],
+        device_id=plane(1), device_id_type=MESH)
     lax.fori_loop(1, ns, send, 0)
     rx[me] = pk[me]
-    lax.fori_loop(1, ns, receive, 0)
+    for c in first_up + first_dn:
+        c.wait_recv()
+    for c in wave2:
+        c.start()
+    packets.wait_recv()
 
     spot = iota((1, LANES), 1)
     power = jnp.left_shift(1, iota((his, LANES), 0)).astype(F32)
@@ -273,9 +308,9 @@
 
     for d in range(1, nm):
         members_copy(d, z).start()
-    for c in up0 + dn1:
+    for c in full_up0 + full_dn1:
         c.wait_recv()
-    for c in up1 + dn0 + fu + fd:
+    for c in wave3:
         c.start()
     for d in range(1, nm):
         members_copy(d, lax.rem(z - d + nm, nm)).wait_recv()
@@ -299,98 +334,115 @@
 
     def to_owner(i):
         return pltpu.make_async_remote_copy(
-            gr.at[i], rbuf.at[me], s1.at[i], r1.at[me],
+            gr.at[i], rbuf.at[me], s1.at[0], r1.at[0],
             device_id={"state": i * stride}, device_id_type=MESH)
 
-    def from_peer(d):
-        src = lax.rem(me + d, ns)
+    def tiles_moved(n, src, dst, ss, rs):
         return pltpu.make_async_remote_copy(
-            gr.at[0], rbuf.at[src], s1.at[0], r1.at[src], device_id=plane(d), device_id_type=MESH)
-
-    def spread_copy(d, i):
-        return pltpu.make_async_remote_copy(
-            gs.at[i], gs.at[i], s2.at[d], r2.at[i], device_id=plane(d), device_id_type=MESH)
+            src.at[pl.ds(0, n)], dst.at[pl.ds(0, n)], ss, rs, device_id=plane(1), device_id_type=MESH)
 
     for i in range(nown):
         @pl.when(me != i * stride)
         def _():
             to_owner(i).start()
 
+    for c in near_up + near_dn + pass_up + pass_dn:
+        c.wait_recv()
+    x4[:, :qc] = jnp.concatenate([e4[:, pl.ds(mid, qc)]] + [q4[r] for r in range(3)], axis=0)
+
     @pl.when(owns)
     def _():
         rbuf[me] = gr[mine]
-
-        def wait_one(d, carry):
-            from_peer(d).wait_recv()
+        tiles_moved(ns - 1, rbuf, rbuf, s1.at[0], r1.at[0]).wait_recv()
+        gs[mine] = jnp.sum(rbuf[...], axis=0)
+
+        def send_one(d, carry):
+            pltpu.make_async_remote_copy(
+                gs.at[mine], gs.at[mine], s2.at[0], r2.at[0],
+                device_id=plane(d), device_id_type=MESH).start()
             return carry
 
-        lax.fori_loop(1, ns, wait_one, 0)
-        gs[mine] = jnp.sum(rbuf[...], axis=0)
-
-        def send_one(d, carry):
-            spread_copy(d, mine).start()
-            return carry
-
         lax.fori_loop(1, ns, send_one, 0)
-
-    for i in range(nown):
-        @pl.when(me != i * stride)
-        def _():
-            spread_copy(1, i).wait_recv()
+        tiles_moved(nown - 1, gs, gs, s2.at[0], r2.at[0]).wait_recv()
+
+    @pl.when(jnp.logical_not(owns))
+    def _():
+        tiles_moved(nown, gs, gs, s2.at[0], r2.at[0]).wait_recv()
 
     mixing = transform(gs[...].reshape(members, LANES), members, yref, zref).astype(BF16)
 
-    rows = 32
-    k = iota((rows, LANES), 0)
-    pick = onehot(jnp.logical_and(iota((rows, LANES), 1) == z * own + k, k < own)).astype(BF16)
     q = iota((members, LANES), 0)
     slot = jnp.where(q < 16 * nm, q // 16, (q - 16 * nm) // (own - 16))
     inner = jnp.where(q < 16 * nm, q % 16, 16 + (q - 16 * nm) % (own - 16))
     dist = jnp.where(slot == 0, 0, jnp.where(slot == 1, nm - 1, slot - 1))
     tab[:members, :LANES] = onehot(iota((members, LANES), 1) == (z + dist) % nm * own + inner).astype(BF16)
     padded = jnp.concatenate([mixing, jnp.zeros((LANES - members, LANES), BF16)], axis=0)
-    mine_t = nt(pick, padded).astype(BF16)
-    mix[...] = nt(mine_t, tab[:members, :LANES]).astype(BF16)
-
-    for c in up0 + dn1:
+    turned = nt(tab[:members, :LANES], padded).astype(BF16)
+    mixp[...] = nt(turned, tab[:members, :LANES]).astype(BF16)
+
+    wide_rows = 16 * nm
+    x = jnp.concatenate([e16[:, pl.ds(mid, qc)]] + [q16[r] for r in range(3)] + [x4[:, :qc]], axis=0)
+    res = jnp.dot(mixp[...], x, preferred_element_type=F32)
+    for t in range(nm):
+        w16[t] = res[16 * t : 16 * (t + 1)].astype(BF16)
+        w4[t] = res[wide_rows + (own - 16) * t : wide_rows + (own - 16) * (t + 1)].astype(BF16)
+    for c in back1:
+        c.start()
+    local = [
+        pltpu.make_async_copy(w16.at[0], out_at(mid, qc)[0], osem.at[0]),
+        pltpu.make_async_copy(w4.at[0], out_at(mid, qc)[1], osem.at[1]),
+    ]
+    for c in local:
+        c.start()
+
+    for c in wave3:
+        c.wait_recv()
+    mine_rows = jnp.concatenate([mixp[:16], mixp[wide_rows:]], axis=0)
+    step = fc // FSTEPS
+    for i in range(FSTEPS):
+        cut = slice(i * step, (i + 1) * step)
+        x = jnp.concatenate(
+            [e16[:, cut]] + [f16[r, :, cut] for r in range(3)]
+            + [e4[:, cut]] + [f4[r, :, cut] for r in range(3)], axis=0)
+        res = jnp.dot(mine_rows, x, preferred_element_type=F32)
+        u16[:, cut] = res[:16].astype(BF16)
+        u4[:, cut] = res[16:own].astype(BF16)
+        if i == FSTEPS // 2 - 1:
+            for c in back_first_up + back_first_dn:
+                c.wait_recv()
+            for c in back2:
+                c.start()
+    more = [
+        pltpu.make_async_copy(u16, out_at(0, fc)[0], osem.at[2]),
+        pltpu.make_async_copy(u4, out_at(0, fc)[1], osem.at[3]),
+    ]
+    for c in more:
+        c.start()
+
+    for c in back_near_up + back_near_dn + back2:
+        c.wait_recv()
+    for c in wave1 + wave2 + wave3 + back1 + back2:
         c.wait_send()
-    for c in up1 + dn0 + fu + fd:
+    for c in local + more:
         c.wait()
-
-    def drain(d, carry):
-        packet(d).wait_send()
-        return carry
-
-    lax.fori_loop(1, ns, drain, 0)
+    packets.wait_send()
     for d in range(1, nm):
         members_copy(d, z).wait_send()
-    for i in range(nown):
-        @pl.when(me != i * stride)
-        def _():
-            to_owner(i).wait_send()
 
     @pl.when(owns)
     def _():
-        def drain2(d, carry):
-            spread_copy(d, mine).wait_send()
-            return carry
-
-        lax.fori_loop(1, ns, drain2, 0)
-
-
-def final(own, ens, g16, g4, mix, out):
-    x = ens[...]
-    parts = [x[:16]] + [g16[r] for r in range(3)]
-    parts.append(jnp.concatenate([x[16:]] + [g4[r] for r in range(3)], axis=0))
-    total = jnp.dot(mix[...], jnp.concatenate(parts, axis=0), preferred_element_type=F32)
-    out[...] = total[:own].astype(BF16)
+        tiles_moved(nown - 1, gr, rbuf, s1.at[0], r1.at[0]).wait_send()
+        tiles_moved(ns - 1, rbuf, rbuf, s2.at[0], r2.at[0]).wait_send()
+
+    @pl.when(jnp.logical_not(owns))
+    def _():
+        tiles_moved(nown, gr, rbuf, s1.at[0], r1.at[0]).wait_send()
 
 
 def per_device(ns, nm, ensemble, weights, seg_obs, observed, inv_var):
     own, cells = ensemble.shape
     tiles, slots, _ = weights.shape
     share = observed.shape[0] // ns
-    route = tiles * slots // ns
     members = own * nm
     nown = 10 if ns >= 10 else 2
     groups = tiles // GT
@@ -400,19 +452,34 @@
     obs = observed.reshape(ns, his, LANES)
     var = inv_var.reshape(ns, his, LANES)
     anyspec = pl.BlockSpec(memory_space=pl.ANY)
-    vspec = pl.BlockSpec(memory_space=pltpu.VMEM)
     dma = pltpu.SemaphoreType.DMA
     col = GT * GT
-    g16, g4, mix = pl.pallas_call(
-        functools.partial(kernel, ns, nm, own, tiles, slots, share, route, nown),
+    fc = cells * FULL // 16
+    qc = (cells - fc) // nm
+    rest = own - 16
+    o16, o4 = pl.pallas_call(
+        functools.partial(kernel, ns, nm, own, tiles, slots, share, nown, fc),
         out_shape=(
-            jax.ShapeDtypeStruct((3, 16, cells), BF16),
-            jax.ShapeDtypeStruct((3, own - 16, cells), BF16),
-            jax.ShapeDtypeStruct((32, members), BF16),
+            jax.ShapeDtypeStruct((16, cells), BF16),
+            jax.ShapeDtypeStruct((rest, cells), BF16),
         ),
         in_specs=[anyspec] * 5,
-        out_specs=(anyspec, anyspec, vspec),
+        out_specs=(anyspec, anyspec),
         scratch_shapes=[
+            pltpu.VMEM((3, 16, fc), BF16),
+            pltpu.VMEM((3, rest, fc), BF16),
+            pltpu.VMEM((3, 16, qc), BF16),
+            pltpu.VMEM((3, rest, qc), BF16),
+            pltpu.VMEM((2, 16, qc // 2), BF16),
+            pltpu.VMEM((2, rest, qc // 2), BF16),
+            pltpu.VMEM((rest * nm, qc), BF16),
+            pltpu.VMEM((nm, 16, qc), BF16),
+            pltpu.VMEM((nm, rest, qc), BF16),
+            pltpu.VMEM((2, 16, qc // 2), BF16),
+            pltpu.VMEM((2, rest, qc // 2), BF16),
+            pltpu.VMEM((16, fc), BF16),
+            pltpu.VMEM((rest, fc), BF16),
+            pltpu.VMEM((members, members), BF16),
             pltpu.VMEM((members, LANES), F32),
             pltpu.VMEM((members, LANES), F32),
             pltpu.VMEM((col, col), BF16),
@@ -436,26 +503,13 @@
             pltpu.VMEM((nown, members // nown, LANES), F32),
             pltpu.VMEM((ns, members // nown, LANES), F32),
             pltpu.VMEM((nown, members // nown, LANES), F32),
-            dma((6,)), dma((12,)), dma((12,)), dma((ns,)), dma((ns,)),
-            dma((nm - 1,)), dma((nm - 1,)), dma((nown,)), dma((ns,)), dma((ns,)), dma((nown,)),
+            dma((6,)), dma((36,)), dma((36,)), dma((1,)), dma((1,)),
+            dma((nm - 1,)), dma((nm - 1,)), dma((1,)), dma((1,)), dma((1,)), dma((1,)), dma((4,)),
         ],
         compiler_params=pltpu.CompilerParams(collective_id=0, has_side_effects=True),
         name="assimilate",
     )(ensemble, wts, ids, obs, var)
-    step = min(4096, cells)
-    return pl.pallas_call(
-        functools.partial(final, own),
-        out_shape=jax.ShapeDtypeStruct((own, cells), BF16),
-        grid=(cells // step,),
-        in_specs=[
-            pl.BlockSpec((own, step), lambda i: (0, i)),
-            pl.BlockSpec((3, 16, step), lambda i: (0, 0, i)),
-            pl.BlockSpec((3, own - 16, step), lambda i: (0, 0, i)),
-            pl.BlockSpec((32, members), lambda i: (0, 0)),
-        ],
-        out_specs=pl.BlockSpec((own, step), lambda i: (0, i)),
-        name="update",
-    )(ensemble, g16, g4, mix)
+    return jnp.concatenate([o16, o4], axis=0)
 
 
 def solution(mesh):

time: 66.7 us -> 59.7 us (0.90)
  the two profiles are of different devices: /device:TPU:1 before, /device:TPU:0 now
where the time goes in v3:
time: 59.7 us; the launch traced here: 59.6 us
  Pallas kernels  57 us (95%)
  other arithmetic  2.59 us (4%)
    pallas_call x1, Pallas kernels, per_device(): pl.pallas_call(functools.partial(kernel, ns, nm, own, tiles, slots, share...  57 us
    concatenate x1, other arithmetic, per_device(): return jnp.concatenate([o16, o4], axis=0)  2.59 us

profile of v3, /device:TPU:0, one launch (start us, length us, event | category | flops | bytes accessed | tf_op | source)
XLA Modules:
  0.0 59.6 jit_solution(15656127208656596355)
XLA Ops:
  0.0 57.0 %assimilate.1 = (bf16[16,32768]{1,0:T(8,128)(2,1)}, bf16[4,32768]{1,0:T(4,128)(2,1)}) custom-call(bf16[20,32768]{1,0:T(8,128)(2,1)} %ens.1, bf16[12,16,16,128]{3,2,1,0:T(8,128)(2,1)} %bitcast.6, s32[12,256]{1,0:T(8,128)} %bitcast.9, f32[32,16,128]{2,1,0:T(8,128)} %bitcast.7, f32[32,16,128]{2,1,0:T(8,128)} %bitcast.8), custom_call_target="tpu_custom_call" | custom-call | tf_op jit(solution)/shard_map/assimilate/pallas_call | solution.py:460
  57.0 2.6 %pad_maximum_fusion = bf16[20,32768]{1,0:T(8,128)(2,1)} fusion(bf16[4,32768]{1,0:T(4,128)(2,1)} %get-tuple-element.8, bf16[16,32768]{1,0:T(8,128)(2,1)} %get-tuple-element.7), kind=kLoop, calls=%fused_computation | loop fusion | flops 2621440 | bytes 2621440 | tf_op jit(solution)/shard_map/concatenate | solution.py:512

commit v4 on v3

--- a/solution.py
+++ b/solution.py
@@ -14,7 +14,7 @@
 GT = 16
 FULL = 8
 FSTEPS = 4
-START = 10
+START = 5
 LANES = 128
 
 
@@ -95,6 +95,10 @@
     chunk = members // nown
     stride = ns // nown
     col = GT * GT
+    two = 2 * GT * slots
+    pairs = groups // 2
+    part = (slots - 8) * GT
+    hw = ns // 2
 
     loads = [
         pltpu.make_async_copy(ens.at[pl.ds(0, 16)], e16, lsem.at[0]),
@@ -158,9 +162,8 @@
     full_dn0 = pair(*own_at(0, fh), *at((f16, f4), 1, 0, fh), dn)
     over_up = pair(*at((f16, f4), 0, 0, fh), *at((f16, f4), 2, 0, fh), up)
     over_dn = pair(*at((f16, f4), 1, fh, fh), *at((f16, f4), 2, fh, fh), dn)
-    wave1 = first_up + first_dn + near_up + near_dn + full_up0 + full_dn1
-    wave2 = pass_up + pass_dn
-    wave3 = full_up1 + full_dn0 + over_up + over_dn
+    wave1 = first_up + first_dn + full_up0 + full_dn1
+    wave2 = near_up + near_dn + pass_up + pass_dn + over_up + over_dn + full_up1 + full_dn0
     mid = pl.multiple_of(fc + z * qc, LANES)
     far = pl.multiple_of(fc + lax.rem(z + 2, nm) * qc, LANES)
 
@@ -180,82 +183,100 @@
 
     loads[3].wait()
     raw = jnp.concatenate([idv[...], jnp.zeros((GT - slots, tiles), I32)], axis=0)
-    tab[:tiles] = onehot(iota((tiles, col), 0) % GT == iota((tiles, col), 1) % GT).astype(BF16)
-    spread = tab[:tiles]
-
-    def regroup(part):
-        part = part.astype(F32)
-        tall = jnp.concatenate(
-            [jnp.where(iota((GT, tiles), 1) // GT == g, part, 0.0) for g in range(groups)], axis=0
+    tab[:tiles, :col] = onehot(iota((tiles, col), 0) % GT == iota((tiles, col), 1) % GT).astype(BF16)
+    spread = tab[:tiles, :col]
+    order = list(range(0, groups, 2)) + list(range(1, groups, 2))
+
+    def regroup(byte):
+        byte = byte.astype(F32)
+        high = jnp.concatenate(
+            [jnp.where(iota((GT, tiles), 1) // GT == g, byte, 0.0) for g in order], axis=0
         ).astype(BF16)
-        out = jnp.dot(tall, spread, preferred_element_type=F32).reshape(groups, GT, col)
-        keep = iota((groups, GT, col), 1) == iota((groups, GT, col), 2) // GT
+        out = jnp.dot(high, spread, preferred_element_type=F32).reshape(groups, GT, col)
+        at_lane = iota((groups, GT, col), 2)
+        shift = jnp.where(jnp.logical_and(iota((groups, GT, col), 0) >= pairs, at_lane >= LANES), part, 0)
+        keep = iota((groups, GT, col), 1) == (at_lane - shift) // GT
         return jnp.sum(jnp.where(keep, out, 0.0), axis=1)
 
-    ident = (regroup(raw // 256) * 256.0 + regroup(raw % 256)).astype(I32)
-    ident = jnp.where(iota((groups, col), 1) < slots * GT, ident, -1)
+    ident = regroup(raw // 256) * 256.0 + regroup(raw % 256)
+    beyond = jnp.where(iota((pairs, LANES), 1) < part, ident[:pairs, LANES:], ident[pairs:, LANES:])
+    ident = jnp.concatenate([ident[:pairs, :LANES], ident[pairs:, :LANES], beyond], axis=1).astype(I32)
     owner = ident // share
-    owner = jnp.where(ident < 0, -1, owner)
     place = ident % share
     code = jnp.left_shift(1, place // LANES).astype(F32) * (1.0 + (place % LANES).astype(F32) / LANES)
 
-    ones = [onehot(iota((ns, col), 0) == owner[g : g + 1]) for g in range(groups)]
-    tab[...] = onehot(iota((col, col), 0) < iota((col, col), 1)).astype(BF16)
-    upper = tab[...]
+    ones = [onehot(iota((ns, two), 0) == owner[g : g + 1]) for g in range(pairs)]
+    tab[...] = onehot(iota((two, two), 0) < iota((two, two), 1)).astype(BF16)
     before = jnp.dot(
-        jnp.concatenate([a.astype(BF16) for a in ones], axis=0), upper, preferred_element_type=F32
+        jnp.concatenate([a.astype(BF16) for a in ones], axis=0), tab[...], preferred_element_type=F32
     )
     run = jnp.zeros((ns, 1), F32)
     ranks = []
-    for g in range(groups):
+    for g in range(pairs):
         rank = jnp.sum(ones[g] * (before[g * ns : (g + 1) * ns] + run), axis=0, keepdims=True)
         run = run + jnp.sum(ones[g], axis=1, keepdims=True)
         rank = rank.astype(I32)
         ranks.append(rank)
-        sel[:, 2 * g * col : (2 * g + 1) * col] = onehot(iota((LANES, col), 0) == rank).astype(BF16)
-        sel[:, (2 * g + 1) * col : (2 * g + 2) * col] = onehot(
-            iota((LANES, col), 0) == LANES - 32 + rank % 32
+        side = owner[g : g + 1] // hw * LANES
+        sel[:, 2 * g * two : (2 * g + 1) * two] = onehot(
+            iota((2 * LANES, two), 0) == rank + side
+        ).astype(BF16)
+        sel[:, (2 * g + 1) * two : (2 * g + 2) * two] = onehot(
+            iota((2 * LANES, two), 0) == LANES - 32 + rank % 32 + side
         ).astype(BF16)
 
     loads[2].wait()
     loads[0].wait()
     loads[1].wait()
     lane = iota((GT, col), 1) % GT
-    row = iota((GT, col), 0)
-    for g in range(groups):
-        w = jnp.concatenate(
-            [wv[:, g].reshape(slots * GT, LANES), jnp.zeros((col - slots * GT, LANES), BF16)], axis=0
-        )
+    lane8 = iota((8, col), 1) % GT - iota((8, col), 0) // 4
+    row = iota((GT, two), 0)
+    gap = jnp.zeros((col - slots * GT, LANES), BF16)
+
+    def values(g):
+        w = wv[:, g].reshape(slots * GT, LANES)
+        if g % 2:
+            w = jnp.concatenate([w[:LANES], gap, w[LANES:]], axis=0)
+        else:
+            w = jnp.concatenate([w, gap], axis=0)
         a = e16[:, g * GT * LANES : (g + 1) * GT * LANES]
         b = e4[:, g * GT * LANES : (g + 1) * GT * LANES]
-        b = jnp.concatenate([b, jnp.zeros((32 - own, GT * LANES), BF16)], axis=0)
-        va16 = nt(jnp.concatenate([a[:, t * LANES : (t + 1) * LANES] for t in range(GT)], axis=0), w)
-        va4 = nt(jnp.concatenate([b[:, t * LANES : (t + 1) * LANES] for t in range(GT)], axis=0), w)
+        a = nt(jnp.concatenate([a[:, t * LANES : (t + 1) * LANES] for t in range(GT)], axis=0), w)
+        b = nt(jnp.concatenate([b[:, t * LANES : (t + 1) * LANES] for t in range(GT)], axis=0), w)
         first = jnp.zeros((GT, col), F32)
-        second = jnp.zeros((GT, col), F32)
+        second = jnp.zeros((8, col), F32)
         for t in range(GT):
-            first = jnp.where(lane == t, va16[t * GT : (t + 1) * GT], first)
-            second = jnp.where(lane == t, va4[t * GT : (t + 1) * GT], second)
+            first = jnp.where(lane == t, a[t * GT : (t + 1) * GT], first)
+        for t in range(0, GT, 2):
+            second = jnp.where(lane8 == t, b[t * 4 : t * 4 + 8], second)
+        return first, second[:4] + second[4:]
+
+    def joined(even, odd):
+        return jnp.concatenate([even[:, :LANES], odd[:, :LANES], even[:, LANES:] + odd[:, LANES:]], axis=1)
+
+    for g in range(pairs):
+        even, odd = values(2 * g), values(2 * g + 1)
+        first, second = joined(even[0], odd[0]), joined(even[1], odd[1])
         extra = [second[r : r + 1] for r in range(own - 16)] + [code[g : g + 1]]
-        rest = jnp.zeros((GT, col), F32)
+        rest = jnp.zeros((GT, two), F32)
         for r, line in enumerate(extra):
             rest = jnp.where(row // 3 == r, line, rest)
         rest = jnp.where(row % 3 == ranks[g] // 32, rest, 0.0)
-        for o in range(ns):
-            there = owner[g : g + 1] == o
-            lhs[o * GT : (o + 1) * GT, :col] = jnp.where(there, first, 0.0).astype(BF16)
-            lhs[o * GT : (o + 1) * GT, col:] = jnp.where(there, rest, 0.0).astype(BF16)
-        part = nt(lhs[...], sel[:, 2 * g * col : (2 * g + 2) * col])
+        for o in range(hw):
+            there = owner[g : g + 1] % hw == o
+            lhs[o * GT : (o + 1) * GT, :two] = jnp.where(there, first, 0.0).astype(BF16)
+            lhs[o * GT : (o + 1) * GT, two:] = jnp.where(there, rest, 0.0).astype(BF16)
+        both = nt(lhs[...], sel[:, 2 * g * two : (2 * g + 2) * two])
         if g == 0:
-            acc[...] = part
+            acc[...] = both
         else:
-            acc[...] += part
-        if g == min(START, groups) - 1:
+            acc[...] += both
+        if g == min(START, pairs) - 1:
             pl.semaphore_wait(barrier, nm - 1 + ns - 1)
             for c in wave1:
                 c.start()
     for o in range(ns):
-        pk[o] = acc[o * GT : (o + 1) * GT, :].astype(BF16)
+        pk[o] = acc[o % hw * GT : (o % hw + 1) * GT, o // hw * LANES : (o // hw + 1) * LANES].astype(BF16)
 
     def send(d, carry):
         pltpu.make_async_remote_copy(
@@ -268,20 +289,16 @@
         device_id=plane(1), device_id_type=MESH)
     lax.fori_loop(1, ns, send, 0)
     rx[me] = pk[me]
-    for c in first_up + first_dn:
-        c.wait_recv()
-    for c in wave2:
-        c.start()
     packets.wait_recv()
 
     spot = iota((1, LANES), 1)
-    power = jnp.left_shift(1, iota((his, LANES), 0)).astype(F32)
-    inverse = jnp.left_shift(1, his - 1 - iota((his, LANES), 0)).astype(F32) * (2.0 ** (1 - his))
-
-    def gather(i, carry):
+    power = jnp.left_shift(1, iota((8, LANES), 0)).astype(F32)
+    inverse = jnp.left_shift(1, 7 - iota((8, LANES), 0)).astype(F32)
+    down = iota((2 * LANES, LANES), 0)
+    for i in range(ns // 8):
         left = []
-        for q in range(4):
-            p = rx[i * 4 + q].astype(F32)
+        for q in range(8):
+            p = rx[i * 8 + q].astype(F32)
             r1x, r2x, r3x = (pltpu.roll(p, 32 * (t + 1), 1) for t in range(3))
             lines = [p[k : k + 1] for k in range(16)]
             for r in range(own - 15):
@@ -289,44 +306,64 @@
                 line = jnp.where(spot < 64, r2x[3 * r + 1 : 3 * r + 2], line)
                 lines.append(jnp.where(spot < 32, r1x[3 * r : 3 * r + 1], line))
             where = lines.pop()
+            upper = where >= 256.0
+            where = jnp.where(upper, where * (1.0 / 256.0), where)
             top = jnp.logical_and(where >= power, where < 2.0 * power)
             left.append(
                 jnp.concatenate([jnp.where(top, v, 0.0) for v in lines], axis=0).astype(BF16)
             )
-            low = where * jnp.sum(jnp.where(top, inverse, 0.0), axis=0, keepdims=True) * LANES - LANES
-            rgt[:, q * LANES : (q + 1) * LANES] = onehot(iota((LANES, LANES), 0).astype(F32) == low).astype(BF16)
-        acc2[...] += nt(jnp.concatenate(left, axis=1), rgt[...])
-        return carry
-
-    acc2[...] = jnp.zeros_like(acc2)
-    lax.fori_loop(0, ns // 4, gather, 0)
+            low = where * jnp.sum(jnp.where(top, inverse, 0.0), axis=0, keepdims=True)
+            low = low.astype(I32) - LANES + jnp.where(upper, LANES, 0)
+            rgt[:, (i * 8 + q) * LANES : (i * 8 + q + 1) * LANES] = onehot(down == low).astype(BF16)
+        both = nt(jnp.concatenate(left, axis=1), rgt[:, i * 8 * LANES : (i + 1) * 8 * LANES])
+        if i == 0:
+            acc2[...] = both
+        else:
+            acc2[...] += both
     hg[z] = acc2[...].astype(BF16)
 
-    def members_copy(d, slot):
+    hrow = own * 8 // 2
+
+    def members_copy(slot, rows, d, n):
+        ref = hg.at[slot, pl.ds(rows * hrow, hrow)]
         return pltpu.make_async_remote_copy(
-            hg.at[z], hg.at[slot], zs.at[d - 1], zr.at[d - 1], device_id=along(d), device_id_type=MESH)
-
-    for d in range(1, nm):
-        members_copy(d, z).start()
-    for c in full_up0 + full_dn1:
+            ref, ref, zs.at[n], zr.at[n], device_id=along(d), device_id_type=MESH)
+
+    before, after = lax.rem(z + dn, nm), lax.rem(z + up, nm)
+    direct = [
+        members_copy(z, 0, up, 0), members_copy(z, 1, dn, 1),
+        members_copy(z, 1, up, 2), members_copy(z, 0, dn, 3),
+    ]
+    passed = [members_copy(before, 0, up, 4), members_copy(after, 1, dn, 5)]
+    for c in direct:
+        c.start()
+    for c, e in zip(direct[:2], passed):
         c.wait_recv()
-    for c in wave3:
+        e.start()
+    for c in first_up + first_dn + full_up0 + full_dn1:
+        c.wait_recv()
+    for c in wave2:
         c.start()
-    for d in range(1, nm):
-        members_copy(d, lax.rem(z - d + nm, nm)).wait_recv()
+    for c in direct[2:] + passed:
+        c.wait_recv()
 
     loads[4].wait()
     loads[5].wait()
-    hf[...] = hg[...].astype(F32).reshape(members * his, LANES)
-    for h in range(his):
-        x = hf[pl.ds(h, members, stride=his), :]
+    rows = members * 8
+    for c in range(2):
+        hf[c * rows : (c + 1) * rows] = hg[:, :, c * LANES : (c + 1) * LANES].astype(F32).reshape(rows, LANES)
+    for h in range(8):
+        x = jnp.concatenate([hf[pl.ds(c * rows + h, members, stride=8), :] for c in range(2)], axis=1)
+        seen = jnp.concatenate([ob[h : h + 1], ob[h + 8 : h + 9]], axis=1)
+        weight = jnp.concatenate([va[h : h + 1], va[h + 8 : h + 9]], axis=1)
         ybar = jnp.sum(x, axis=0, keepdims=True) / members
         dev = x - ybar
-        an[:members, h * LANES : (h + 1) * LANES] = dev
-        an[members:, h * LANES : (h + 1) * LANES] = jnp.where(
-            iota((LANES - members, LANES), 0) == 0, ob[h : h + 1] - ybar, 0.0
+        cut = slice(h * 2 * LANES, (h + 1) * 2 * LANES)
+        an[:members, cut] = dev
+        an[members:, cut] = jnp.where(
+            iota((LANES - members, 2 * LANES), 0) == 0, seen - ybar, 0.0
         )
-        wa[:, h * LANES : (h + 1) * LANES] = dev * va[h : h + 1]
+        wa[:, cut] = dev * weight
     gr[...] = nt(wa[...], an[...], lax.Precision.HIGHEST).reshape(nown, chunk, LANES)
 
     mine = me // stride
@@ -395,7 +432,7 @@
     for c in local:
         c.start()
 
-    for c in wave3:
+    for c in over_up + over_dn + full_up1 + full_dn0:
         c.wait_recv()
     mine_rows = jnp.concatenate([mixp[:16], mixp[wide_rows:]], axis=0)
     step = fc // FSTEPS
@@ -421,13 +458,11 @@
 
     for c in back_near_up + back_near_dn + back2:
         c.wait_recv()
-    for c in wave1 + wave2 + wave3 + back1 + back2:
+    for c in wave1 + wave2 + back1 + back2 + direct + passed:
         c.wait_send()
     for c in local + more:
         c.wait()
     packets.wait_send()
-    for d in range(1, nm):
-        members_copy(d, z).wait_send()
 
     @pl.when(owns)
     def _():
@@ -453,7 +488,7 @@
     var = inv_var.reshape(ns, his, LANES)
     anyspec = pl.BlockSpec(memory_space=pl.ANY)
     dma = pltpu.SemaphoreType.DMA
-    col = GT * GT
+    two = 2 * GT * slots
     fc = cells * FULL // 16
     qc = (cells - fc) // nm
     rest = own - 16
@@ -482,29 +517,29 @@
             pltpu.VMEM((members, members), BF16),
             pltpu.VMEM((members, LANES), F32),
             pltpu.VMEM((members, LANES), F32),
-            pltpu.VMEM((col, col), BF16),
-            pltpu.VMEM((LANES, 4 * LANES), BF16),
+            pltpu.VMEM((two, two), BF16),
+            pltpu.VMEM((2 * LANES, ns * LANES), BF16),
             pltpu.VMEM((16, cells), BF16),
             pltpu.VMEM((own - 16, cells), BF16),
             pltpu.VMEM((slots, groups, GT, LANES), BF16),
             pltpu.VMEM((slots, tiles), I32),
             pltpu.VMEM((his, LANES), F32),
             pltpu.VMEM((his, LANES), F32),
-            pltpu.VMEM((ns * GT, 2 * col), BF16),
-            pltpu.VMEM((LANES, 2 * groups * col), BF16),
-            pltpu.VMEM((ns * GT, LANES), F32),
+            pltpu.VMEM((ns // 2 * GT, 2 * two), BF16),
+            pltpu.VMEM((2 * LANES, groups * two), BF16),
+            pltpu.VMEM((ns // 2 * GT, 2 * LANES), F32),
             pltpu.VMEM((ns, GT, LANES), BF16),
             pltpu.VMEM((ns, GT, LANES), BF16),
-            pltpu.VMEM((own * his, LANES), F32),
-            pltpu.VMEM((nm, own * his, LANES), BF16),
-            pltpu.VMEM((members * his, LANES), F32),
+            pltpu.VMEM((own * 8, 2 * LANES), F32),
+            pltpu.VMEM((nm, own * 8, 2 * LANES), BF16),
+            pltpu.VMEM((2 * members * 8, LANES), F32),
             pltpu.VMEM((LANES, share), F32),
             pltpu.VMEM((members, share), F32),
             pltpu.VMEM((nown, members // nown, LANES), F32),
             pltpu.VMEM((ns, members // nown, LANES), F32),
             pltpu.VMEM((nown, members // nown, LANES), F32),
             dma((6,)), dma((36,)), dma((36,)), dma((1,)), dma((1,)),
-            dma((nm - 1,)), dma((nm - 1,)), dma((1,)), dma((1,)), dma((1,)), dma((1,)), dma((4,)),
+            dma((6,)), dma((6,)), dma((1,)), dma((1,)), dma((1,)), dma((1,)), dma((4,)),
         ],
         compiler_params=pltpu.CompilerParams(collective_id=0, has_side_effects=True),
         name="assimilate",

time: 59.7 us -> 55.6 us (0.931)
  the two profiles are of different devices: /device:TPU:0 before, /device:TPU:1 now
where the time goes in v4:
time: 55.6 us; the launch traced here: 55.5 us
  Pallas kernels  52.9 us (95%)
  other arithmetic  2.59 us (5%)
    pallas_call x1, Pallas kernels, per_device(): pl.pallas_call(functools.partial(kernel, ns, nm, own, tiles, slots, share...  52.9 us
    concatenate x1, other arithmetic, per_device(): return jnp.concatenate([o16, o4], axis=0)  2.59 us

profile of v4, /device:TPU:1, one launch (start us, length us, event | category | flops | bytes accessed | tf_op | source)
XLA Modules:
  0.0 55.5 jit_solution(9478852390048067253)
XLA Ops:
  0.0 52.9 %assimilate.1 = (bf16[16,32768]{1,0:T(8,128)(2,1)}, bf16[4,32768]{1,0:T(4,128)(2,1)}) custom-call(bf16[20,32768]{1,0:T(8,128)(2,1)} %ens.1, bf16[12,16,16,128]{3,2,1,0:T(8,128)(2,1)} %bitcast.6, s32[12,256]{1,0:T(8,128)} %bitcast.9, f32[32,16,128]{2,1,0:T(8,128)} %bitcast.7, f32[32,16,128]{2,1,0:T(8,128)} %bitcast.8), custom_call_target="tpu_custom_call" | custom-call | tf_op jit(solution)/shard_map/assimilate/pallas_call | solution.py:495
  52.9 2.6 %pad_maximum_fusion = bf16[20,32768]{1,0:T(8,128)(2,1)} fusion(bf16[4,32768]{1,0:T(4,128)(2,1)} %get-tuple-element.8, bf16[16,32768]{1,0:T(8,128)(2,1)} %get-tuple-element.7), kind=kLoop, calls=%fused_computation | loop fusion | flops 2621440 | bytes 2621440 | tf_op jit(solution)/shard_map/concatenate | solution.py:547

commit v5 on v4

--- a/solution.py
+++ b/solution.py
@@ -81,9 +81,9 @@
     ns, nm, own, tiles, slots, share, nown, fc,
     ens, wts, ids, obs, var,
     o16, o4,
-    f16, f4, q16, q4, t16, t4, x4, w16, w4, v16, v4, u16, u4, mixp,
+    f16, f4, q16, q4, t16, t4, x4, w16, w4, v16, v4, mixp,
     yref, zref, tab, rgt, e16, e4, wv, idv, ob, va, lhs, sel, acc, pk, rx, acc2, hg, hf, an, wa, gr, rbuf, gs,
-    lsem, bs, br, ps, pr, zs, zr, s1, r1, s2, r2, osem,
+    lsem, bs, br, ps, pr, zs, zr, s1, r1, s2, r2,
 ):
     me = lax.axis_index("state")
     z = lax.axis_index("mem")
@@ -420,16 +420,12 @@
     wide_rows = 16 * nm
     x = jnp.concatenate([e16[:, pl.ds(mid, qc)]] + [q16[r] for r in range(3)] + [x4[:, :qc]], axis=0)
     res = jnp.dot(mixp[...], x, preferred_element_type=F32)
-    for t in range(nm):
+    o16[:, pl.ds(mid, qc)] = res[:16].astype(BF16)
+    o4[:, pl.ds(mid, qc)] = res[wide_rows : wide_rows + own - 16].astype(BF16)
+    for t in range(1, nm):
         w16[t] = res[16 * t : 16 * (t + 1)].astype(BF16)
         w4[t] = res[wide_rows + (own - 16) * t : wide_rows + (own - 16) * (t + 1)].astype(BF16)
     for c in back1:
-        c.start()
-    local = [
-        pltpu.make_async_copy(w16.at[0], out_at(mid, qc)[0], osem.at[0]),
-        pltpu.make_async_copy(w4.at[0], out_at(mid, qc)[1], osem.at[1]),
-    ]
-    for c in local:
         c.start()
 
     for c in over_up + over_dn + full_up1 + full_dn0:
@@ -442,26 +438,17 @@
             [e16[:, cut]] + [f16[r, :, cut] for r in range(3)]
             + [e4[:, cut]] + [f4[r, :, cut] for r in range(3)], axis=0)
         res = jnp.dot(mine_rows, x, preferred_element_type=F32)
-        u16[:, cut] = res[:16].astype(BF16)
-        u4[:, cut] = res[16:own].astype(BF16)
+        o16[:, cut] = res[:16].astype(BF16)
+        o4[:, cut] = res[16:own].astype(BF16)
         if i == FSTEPS // 2 - 1:
             for c in back_first_up + back_first_dn:
                 c.wait_recv()
             for c in back2:
                 c.start()
-    more = [
-        pltpu.make_async_copy(u16, out_at(0, fc)[0], osem.at[2]),
-        pltpu.make_async_copy(u4, out_at(0, fc)[1], osem.at[3]),
-    ]
-    for c in more:
-        c.start()
-
     for c in back_near_up + back_near_dn + back2:
         c.wait_recv()
     for c in wave1 + wave2 + back1 + back2 + direct + passed:
         c.wait_send()
-    for c in local + more:
-        c.wait()
     packets.wait_send()
 
     @pl.when(owns)
@@ -488,6 +475,7 @@
     var = inv_var.reshape(ns, his, LANES)
     anyspec = pl.BlockSpec(memory_space=pl.ANY)
     dma = pltpu.SemaphoreType.DMA
+    vspec = pl.BlockSpec(memory_space=pltpu.VMEM)
     two = 2 * GT * slots
     fc = cells * FULL // 16
     qc = (cells - fc) // nm
@@ -495,11 +483,11 @@
     o16, o4 = pl.pallas_call(
         functools.partial(kernel, ns, nm, own, tiles, slots, share, nown, fc),
         out_shape=(
-            jax.ShapeDtypeStruct((16, cells), BF16),
-            jax.ShapeDtypeStruct((rest, cells), BF16),
+            pltpu.VMEM((16, cells), BF16),
+            pltpu.VMEM((rest, cells), BF16),
         ),
         in_specs=[anyspec] * 5,
-        out_specs=(anyspec, anyspec),
+        out_specs=(vspec, vspec),
         scratch_shapes=[
             pltpu.VMEM((3, 16, fc), BF16),
             pltpu.VMEM((3, rest, fc), BF16),
@@ -512,8 +500,6 @@
             pltpu.VMEM((nm, rest, qc), BF16),
             pltpu.VMEM((2, 16, qc // 2), BF16),
             pltpu.VMEM((2, rest, qc // 2), BF16),
-            pltpu.VMEM((16, fc), BF16),
-            pltpu.VMEM((rest, fc), BF16),
             pltpu.VMEM((members, members), BF16),
             pltpu.VMEM((members, LANES), F32),
             pltpu.VMEM((members, LANES), F32),
@@ -539,12 +525,29 @@
             pltpu.VMEM((ns, members // nown, LANES), F32),
             pltpu.VMEM((nown, members // nown, LANES), F32),
             dma((6,)), dma((36,)), dma((36,)), dma((1,)), dma((1,)),
-            dma((6,)), dma((6,)), dma((1,)), dma((1,)), dma((1,)), dma((1,)), dma((4,)),
+            dma((6,)), dma((6,)), dma((1,)), dma((1,)), dma((1,)), dma((1,)),
         ],
         compiler_params=pltpu.CompilerParams(collective_id=0, has_side_effects=True),
         name="assimilate",
     )(ensemble, wts, ids, obs, var)
-    return jnp.concatenate([o16, o4], axis=0)
+    def settle(o16_ref, o4_ref, out, sem):
+        moves = [
+            pltpu.make_async_copy(o16_ref, out.at[pl.ds(0, 16)], sem.at[0]),
+            pltpu.make_async_copy(o4_ref, out.at[pl.ds(16, rest)], sem.at[1]),
+        ]
+        for c in moves:
+            c.start()
+        for c in moves:
+            c.wait()
+
+    return pl.pallas_call(
+        settle,
+        out_shape=jax.ShapeDtypeStruct((own, cells), BF16),
+        in_specs=[vspec] * 2,
+        out_specs=anyspec,
+        scratch_shapes=[dma((2,))],
+        name="settle",
+    )(*(pltpu.with_memory_space_constraint(o, pltpu.VMEM) for o in (o16, o4)))
 
 
 def solution(mesh):

time: 55.6 us -> 54 us (0.971)
  other arithmetic: 2.59 us -> 0 us
  Pallas kernels: 52.9 us -> 53.8 us
    concatenate x1 -> x0, other arithmetic: 2.59 us -> none  [per_device(): return jnp.concatenate([o16, o4], axis=0)]
    pallas_call x0 -> x1, Pallas kernels: none -> 1.07 us  [per_device(): pl.pallas_call(settle, out_shape=jax.ShapeDtypeStruct((own, cells), BF16)...]
where the time goes in v5:
time: 54 us; the launch traced here: 53.8 us
  Pallas kernels  53.8 us (100%)
    pallas_call x1, Pallas kernels, per_device(): pl.pallas_call(functools.partial(kernel, ns, nm, own, tiles, slots, share...  52.8 us

profile of v5, /device:TPU:1, one launch (start us, length us, event | category | flops | bytes accessed | tf_op | source)
XLA Modules:
  0.0 53.8 jit_solution(7405132131356477731)
XLA Ops:
  0.0 52.8 %assimilate.1 = (bf16[16,32768]{1,0:T(8,128)(2,1)S(1)}, bf16[4,32768]{1,0:T(4,128)(2,1)S(1)}) custom-call(bf16[20,32768]{1,0:T(8,128)(2,1)} %ens.1, bf16[12,16,16,128]{3,2,1,0:T(8,128)(2,1)} %bitcast.6, s32[12,256]{1,0:T(8,128)} %bitcast.9, f32[32,16,128]{2,1,0:T(8,128)} %bitcast.7, f32[32,16,128]{2,1,0:T(8,128)} %bitcast.8), custom_call_target="tpu_custom_call" | custom-call | tf_op jit(solution)/shard_map/assimilate/pallas_call | solution.py:483
  52.8 1.1 %settle.1 = bf16[20,32768]{1,0:T(8,128)(2,1)} custom-call(bf16[16,32768]{1,0:T(8,128)(2,1)S(1)} %get-tuple-element.7.o16_ref, bf16[4,32768]{1,0:T(4,128)(2,1)S(1)} %get-tuple-element.8.o4_ref), custom_call_target="tpu_custom_call" | custom-call | tf_op jit(solution)/shard_map/settle/pallas_call | solution.py:543

commit v6 on v5

--- a/solution.py
+++ b/solution.py
@@ -12,8 +12,9 @@
 F32, BF16, I32 = jnp.float32, jnp.bfloat16, jnp.int32
 MESH = pl.DeviceIdType.MESH
 GT = 16
-FULL = 8
+FULL = 9
 FSTEPS = 4
+BATCH = 4
 START = 5
 LANES = 128
 
@@ -211,26 +212,20 @@
         jnp.concatenate([a.astype(BF16) for a in ones], axis=0), tab[...], preferred_element_type=F32
     )
     run = jnp.zeros((ns, 1), F32)
-    ranks = []
     for g in range(pairs):
         rank = jnp.sum(ones[g] * (before[g * ns : (g + 1) * ns] + run), axis=0, keepdims=True)
         run = run + jnp.sum(ones[g], axis=1, keepdims=True)
         rank = rank.astype(I32)
-        ranks.append(rank)
         side = owner[g : g + 1] // hw * LANES
-        sel[:, 2 * g * two : (2 * g + 1) * two] = onehot(
-            iota((2 * LANES, two), 0) == rank + side
-        ).astype(BF16)
-        sel[:, (2 * g + 1) * two : (2 * g + 2) * two] = onehot(
-            iota((2 * LANES, two), 0) == LANES - 32 + rank % 32 + side
-        ).astype(BF16)
+        sel[:, g * two : (g + 1) * two] = onehot(iota((2 * LANES, two), 0) == rank + side).astype(BF16)
 
     loads[2].wait()
     loads[0].wait()
     loads[1].wait()
     lane = iota((GT, col), 1) % GT
     lane8 = iota((8, col), 1) % GT - iota((8, col), 0) // 4
-    row = iota((GT, two), 0)
+    row = iota((8, two), 0)
+    split_at = hw * GT
     gap = jnp.zeros((col - slots * GT, LANES), BF16)
 
     def values(g):
@@ -257,26 +252,39 @@
     for g in range(pairs):
         even, odd = values(2 * g), values(2 * g + 1)
         first, second = joined(even[0], odd[0]), joined(even[1], odd[1])
-        extra = [second[r : r + 1] for r in range(own - 16)] + [code[g : g + 1]]
-        rest = jnp.zeros((GT, two), F32)
-        for r, line in enumerate(extra):
-            rest = jnp.where(row // 3 == r, line, rest)
-        rest = jnp.where(row % 3 == ranks[g] // 32, rest, 0.0)
+        rest = jnp.concatenate([second, jnp.zeros((20 - own + 4, two), F32)], axis=0)
+        rest = jnp.where(row == own - 16, code[g : g + 1], rest)
+        here = slice(g * two, (g + 1) * two)
         for o in range(hw):
             there = owner[g : g + 1] % hw == o
-            lhs[o * GT : (o + 1) * GT, :two] = jnp.where(there, first, 0.0).astype(BF16)
-            lhs[o * GT : (o + 1) * GT, two:] = jnp.where(there, rest, 0.0).astype(BF16)
-        both = nt(lhs[...], sel[:, 2 * g * two : (2 * g + 2) * two])
-        if g == 0:
-            acc[...] = both
-        else:
-            acc[...] += both
+            lhs[o * GT : (o + 1) * GT, here] = jnp.where(there, first, 0.0).astype(BF16)
+        for o in range(0, hw, 2):
+            low = jnp.where(owner[g : g + 1] % hw == o, rest, 0.0)
+            high = jnp.where(owner[g : g + 1] % hw == o + 1, rest, 0.0)
+            lhs[split_at + o * 8 : split_at + o * 8 + 16, here] = jnp.concatenate(
+                [low, high], axis=0
+            ).astype(BF16)
+        if g % BATCH == BATCH - 1:
+            cut = slice((g + 1 - BATCH) * two, (g + 1) * two)
+            both = nt(lhs[:, cut], sel[:, cut])
+            if g == BATCH - 1:
+                acc[...] = both
+            else:
+                acc[...] += both
         if g == min(START, pairs) - 1:
             pl.semaphore_wait(barrier, nm - 1 + ns - 1)
             for c in wave1:
                 c.start()
+    eight = iota((8, LANES), 0)
+    spot = iota((1, LANES), 1)
     for o in range(ns):
-        pk[o] = acc[o % hw * GT : (o % hw + 1) * GT, o // hw * LANES : (o // hw + 1) * LANES].astype(BF16)
+        across = slice(o // hw * LANES, (o // hw + 1) * LANES)
+        main = acc[o % hw * GT : (o % hw + 1) * GT, across]
+        rest = acc[split_at + o % hw * 8 : split_at + (o % hw + 1) * 8, across]
+        p0, p1, p2 = (pltpu.roll(rest, 96 - 32 * t, 1) for t in range(3))
+        head = jnp.where(eight < 5, p0, pltpu.roll(p2, 5, 0))
+        tail = jnp.where(eight < 5, p1, pltpu.roll(p2, 2, 0))
+        pk[o] = jnp.where(spot < 96, main, jnp.concatenate([head, tail], axis=0)).astype(BF16)
 
     def send(d, carry):
         pltpu.make_async_remote_copy(
@@ -302,9 +310,10 @@
             r1x, r2x, r3x = (pltpu.roll(p, 32 * (t + 1), 1) for t in range(3))
             lines = [p[k : k + 1] for k in range(16)]
             for r in range(own - 15):
-                line = jnp.where(spot < 96, r3x[3 * r + 2 : 3 * r + 3], 0.0)
-                line = jnp.where(spot < 64, r2x[3 * r + 1 : 3 * r + 2], line)
-                lines.append(jnp.where(spot < 32, r1x[3 * r : 3 * r + 1], line))
+                third = 5 + r if r < 3 else 10 + r
+                line = jnp.where(spot < 96, r3x[third : third + 1], 0.0)
+                line = jnp.where(spot < 64, r2x[8 + r : 9 + r], line)
+                lines.append(jnp.where(spot < 32, r1x[r : r + 1], line))
             where = lines.pop()
             upper = where >= 256.0
             where = jnp.where(upper, where * (1.0 / 256.0), where)
@@ -511,9 +520,9 @@
             pltpu.VMEM((slots, tiles), I32),
             pltpu.VMEM((his, LANES), F32),
             pltpu.VMEM((his, LANES), F32),
-            pltpu.VMEM((ns // 2 * GT, 2 * two), BF16),
-            pltpu.VMEM((2 * LANES, groups * two), BF16),
-            pltpu.VMEM((ns // 2 * GT, 2 * LANES), F32),
+            pltpu.VMEM((ns // 2 * (GT + 8), groups // 2 * two), BF16),
+            pltpu.VMEM((2 * LANES, groups // 2 * two), BF16),
+            pltpu.VMEM((ns // 2 * (GT + 8), 2 * LANES), F32),
             pltpu.VMEM((ns, GT, LANES), BF16),
             pltpu.VMEM((ns, GT, LANES), BF16),
             pltpu.VMEM((own * 8, 2 * LANES), F32),

time: 54 us -> 53.6 us (level); the launches traced: 53.8 us -> 52.6 us
  Pallas kernels: 53.8 us -> 52.6 us
    pallas_call x1, Pallas kernels: 52.8 us -> 51.5 us  [per_device(): pl.pallas_call(functools.partial(kernel, ns, nm, own, tiles, slots, share...]
where the time goes in v6:
time: 53.6 us; the launch traced here: 52.6 us
  Pallas kernels  52.6 us (98%)
    pallas_call x1, Pallas kernels, per_device(): pl.pallas_call(functools.partial(kernel, ns, nm, own, tiles, slots, share...  51.5 us

profile of v6, /device:TPU:1, one launch (start us, length us, event | category | flops | bytes accessed | tf_op | source)
XLA Modules:
  0.0 52.6 jit_solution(13745392541550946187)
XLA Ops:
  0.0 51.5 %assimilate.1 = (bf16[16,32768]{1,0:T(8,128)(2,1)S(1)}, bf16[4,32768]{1,0:T(4,128)(2,1)S(1)}) custom-call(bf16[20,32768]{1,0:T(8,128)(2,1)} %ens.1, bf16[12,16,16,128]{3,2,1,0:T(8,128)(2,1)} %bitcast.6, s32[12,256]{1,0:T(8,128)} %bitcast.9, f32[32,16,128]{2,1,0:T(8,128)} %bitcast.7, f32[32,16,128]{2,1,0:T(8,128)} %bitcast.8), custom_call_target="tpu_custom_call" | custom-call | tf_op jit(solution)/shard_map/assimilate/pallas_call | solution.py:492
  51.5 1.1 %settle.1 = bf16[20,32768]{1,0:T(8,128)(2,1)} custom-call(bf16[16,32768]{1,0:T(8,128)(2,1)S(1)} %get-tuple-element.7.o16_ref, bf16[4,32768]{1,0:T(4,128)(2,1)S(1)} %get-tuple-element.8.o4_ref), custom_call_target="tpu_custom_call" | custom-call | tf_op jit(solution)/shard_map/settle/pallas_call | solution.py:552

commit v7 on v6

--- a/solution.py
+++ b/solution.py
@@ -12,7 +12,7 @@
 F32, BF16, I32 = jnp.float32, jnp.bfloat16, jnp.int32
 MESH = pl.DeviceIdType.MESH
 GT = 16
-FULL = 9
+FULL = 7
 FSTEPS = 4
 BATCH = 4
 START = 5
@@ -59,8 +59,10 @@
     identity = onehot(down == across)
     system = (members - 1.0) * identity + jnp.where(across < members, total, 0.0)
     scaling = jnp.sqrt(jnp.sum(jnp.sum(system * system, axis=1, keepdims=True), axis=0, keepdims=True))
-    yref[...] = system / scaling
-    zref[...] = identity
+    y = system / scaling
+    c = 1.5 * identity - 0.5 * y
+    yref[...] = product(wide(y), tall(c))
+    zref[...] = c
 
     def step(_, carry):
         y, z = yref[...], zref[...]
@@ -69,7 +71,7 @@
         zref[...] = product(wide(c), tall(z))
         return carry
 
-    lax.fori_loop(0, ITERS, step, 0)
+    lax.fori_loop(1, ITERS, step, 0)
     root = zref[...] / jnp.sqrt(scaling)
     left = wide(root)
     twice = product(left, tall(product(left, tall(total))))
@@ -82,7 +84,7 @@
     ns, nm, own, tiles, slots, share, nown, fc,
     ens, wts, ids, obs, var,
     o16, o4,
-    f16, f4, q16, q4, t16, t4, x4, w16, w4, v16, v4, mixp,
+    f16, f4, q16, q4, t16, t4, x4, w16, w4, mixp,
     yref, zref, tab, rgt, e16, e4, wv, idv, ob, va, lhs, sel, acc, pk, rx, acc2, hg, hf, an, wa, gr, rbuf, gs,
     lsem, bs, br, ps, pr, zs, zr, s1, r1, s2, r2,
 ):
@@ -164,23 +166,18 @@
     over_up = pair(*at((f16, f4), 0, 0, fh), *at((f16, f4), 2, 0, fh), up)
     over_dn = pair(*at((f16, f4), 1, fh, fh), *at((f16, f4), 2, fh, fh), dn)
     wave1 = first_up + first_dn + full_up0 + full_dn1
-    wave2 = near_up + near_dn + pass_up + pass_dn + over_up + over_dn + full_up1 + full_dn0
+    wave2 = near_up + near_dn + pass_up + pass_dn + full_up1 + full_dn0
+    wave3 = over_up + over_dn
     mid = pl.multiple_of(fc + z * qc, LANES)
     far = pl.multiple_of(fc + lax.rem(z + 2, nm) * qc, LANES)
 
     def out_at(start, n):
         return o16.at[:, pl.ds(start, n)], o4.at[:, pl.ds(start, n)]
 
-    back_first_up = pair(*at((w16, w4), 3, 0, qh), *at((v16, v4), 0, 0, qh), up)
-    back_first_dn = pair(*at((w16, w4), 3, qh, qh), *at((v16, v4), 1, 0, qh), dn)
+    back_far = pair(*at((w16, w4), 3, 0, qc), *out_at(mid, qc), 2)
     back_near_up = pair(*at((w16, w4), 2, 0, qc), *out_at(mid, qc), up)
     back_near_dn = pair(*at((w16, w4), 1, 0, qc), *out_at(mid, qc), dn)
-    before_mid = pl.multiple_of(fc + lax.rem(z + dn, nm) * qc, LANES)
-    after_mid = pl.multiple_of(fc + lax.rem(z + up, nm) * qc, LANES)
-    back_pass_up = pair(*at((v16, v4), 0, 0, qh), *out_at(before_mid, qh), up)
-    back_pass_dn = pair(*at((v16, v4), 1, 0, qh), *out_at(after_mid + qh, qh), dn)
-    back1 = back_first_up + back_first_dn + back_near_up + back_near_dn
-    back2 = back_pass_up + back_pass_dn
+    back1 = back_far + back_near_up + back_near_dn
 
     loads[3].wait()
     raw = jnp.concatenate([idv[...], jnp.zeros((GT - slots, tiles), I32)], axis=0)
@@ -331,29 +328,19 @@
             acc2[...] += both
     hg[z] = acc2[...].astype(BF16)
 
-    hrow = own * 8 // 2
-
-    def members_copy(slot, rows, d, n):
-        ref = hg.at[slot, pl.ds(rows * hrow, hrow)]
+    def members_copy(d, n):
+        ref = hg.at[z]
         return pltpu.make_async_remote_copy(
             ref, ref, zs.at[n], zr.at[n], device_id=along(d), device_id_type=MESH)
 
-    before, after = lax.rem(z + dn, nm), lax.rem(z + up, nm)
-    direct = [
-        members_copy(z, 0, up, 0), members_copy(z, 1, dn, 1),
-        members_copy(z, 1, up, 2), members_copy(z, 0, dn, 3),
-    ]
-    passed = [members_copy(before, 0, up, 4), members_copy(after, 1, dn, 5)]
+    direct = [members_copy(2, 0), members_copy(up, 1), members_copy(dn, 2)]
     for c in direct:
         c.start()
-    for c, e in zip(direct[:2], passed):
-        c.wait_recv()
-        e.start()
-    for c in first_up + first_dn + full_up0 + full_dn1:
+    for c in first_up + first_dn:
         c.wait_recv()
     for c in wave2:
         c.start()
-    for c in direct[2:] + passed:
+    for c in direct:
         c.wait_recv()
 
     loads[4].wait()
@@ -392,6 +379,10 @@
         def _():
             to_owner(i).start()
 
+    for c in full_up0 + full_dn1:
+        c.wait_recv()
+    for c in wave3:
+        c.start()
     for c in near_up + near_dn + pass_up + pass_dn:
         c.wait_recv()
     x4[:, :qc] = jnp.concatenate([e4[:, pl.ds(mid, qc)]] + [q4[r] for r in range(3)], axis=0)
@@ -427,13 +418,16 @@
     mixp[...] = nt(turned, tab[:members, :LANES]).astype(BF16)
 
     wide_rows = 16 * nm
-    x = jnp.concatenate([e16[:, pl.ds(mid, qc)]] + [q16[r] for r in range(3)] + [x4[:, :qc]], axis=0)
-    res = jnp.dot(mixp[...], x, preferred_element_type=F32)
-    o16[:, pl.ds(mid, qc)] = res[:16].astype(BF16)
-    o4[:, pl.ds(mid, qc)] = res[wide_rows : wide_rows + own - 16].astype(BF16)
-    for t in range(1, nm):
-        w16[t] = res[16 * t : 16 * (t + 1)].astype(BF16)
-        w4[t] = res[wide_rows + (own - 16) * t : wide_rows + (own - 16) * (t + 1)].astype(BF16)
+    for part in range(2):
+        here = slice(part * qh, (part + 1) * qh)
+        at_mid = pl.ds(pl.multiple_of(mid + part * qh, LANES), qh)
+        x = jnp.concatenate([e16[:, at_mid]] + [q16[r, :, here] for r in range(3)] + [x4[:, here]], axis=0)
+        res = jnp.dot(mixp[...], x, preferred_element_type=F32)
+        for t in range(nm - 1, 0, -1):
+            w16[t, :, here] = res[16 * t : 16 * (t + 1)].astype(BF16)
+            w4[t, :, here] = res[wide_rows + (own - 16) * t : wide_rows + (own - 16) * (t + 1)].astype(BF16)
+        o16[:, at_mid] = res[:16].astype(BF16)
+        o4[:, at_mid] = res[wide_rows : wide_rows + own - 16].astype(BF16)
     for c in back1:
         c.start()
 
@@ -449,14 +443,10 @@
         res = jnp.dot(mine_rows, x, preferred_element_type=F32)
         o16[:, cut] = res[:16].astype(BF16)
         o4[:, cut] = res[16:own].astype(BF16)
-        if i == FSTEPS // 2 - 1:
-            for c in back_first_up + back_first_dn:
-                c.wait_recv()
-            for c in back2:
-                c.start()
-    for c in back_near_up + back_near_dn + back2:
+
+    for c in back1:
         c.wait_recv()
-    for c in wave1 + wave2 + back1 + back2 + direct + passed:
+    for c in wave1 + wave2 + wave3 + back1 + direct:
         c.wait_send()
     packets.wait_send()
 
@@ -507,8 +497,6 @@
             pltpu.VMEM((rest * nm, qc), BF16),
             pltpu.VMEM((nm, 16, qc), BF16),
             pltpu.VMEM((nm, rest, qc), BF16),
-            pltpu.VMEM((2, 16, qc // 2), BF16),
-            pltpu.VMEM((2, rest, qc // 2), BF16),
             pltpu.VMEM((members, members), BF16),
             pltpu.VMEM((members, LANES), F32),
             pltpu.VMEM((members, LANES), F32),
@@ -534,7 +522,7 @@
             pltpu.VMEM((ns, members // nown, LANES), F32),
             pltpu.VMEM((nown, members // nown, LANES), F32),
             dma((6,)), dma((36,)), dma((36,)), dma((1,)), dma((1,)),
-            dma((6,)), dma((6,)), dma((1,)), dma((1,)), dma((1,)), dma((1,)),
+            dma((3,)), dma((3,)), dma((1,)), dma((1,)), dma((1,)), dma((1,)),
         ],
         compiler_params=pltpu.CompilerParams(collective_id=0, has_side_effects=True),
         name="assimilate",

time: 53.6 us -> 51.6 us (0.963); the launches traced: 52.6 us -> 51.4 us
  Pallas kernels: 52.6 us -> 51.4 us
    pallas_call x1, Pallas kernels: 51.5 us -> 50.3 us  [per_device(): pl.pallas_call(functools.partial(kernel, ns, nm, own, tiles, slots, share...]
where the time goes in v7:
time: 51.6 us; the launch traced here: 51.4 us
  Pallas kernels  51.4 us (100%)
    pallas_call x1, Pallas kernels, per_device(): pl.pallas_call(functools.partial(kernel, ns, nm, own, tiles, slots, share...  50.3 us
    pallas_call x1, Pallas kernels, per_device(): pl.pallas_call(settle, out_shape=jax.ShapeDtypeStruct((own, cells), BF16)...  1.07 us

profile of v7, /device:TPU:1, one launch (start us, length us, event | category | flops | bytes accessed | tf_op | source)
XLA Modules:
  0.0 51.4 jit_solution(1138242881955058468)
XLA Ops:
  0.0 50.3 %assimilate.1 = (bf16[16,32768]{1,0:T(8,128)(2,1)S(1)}, bf16[4,32768]{1,0:T(4,128)(2,1)S(1)}) custom-call(bf16[20,32768]{1,0:T(8,128)(2,1)} %ens.1, bf16[12,16,16,128]{3,2,1,0:T(8,128)(2,1)} %bitcast.6, s32[12,256]{1,0:T(8,128)} %bitcast.9, f32[32,16,128]{2,1,0:T(8,128)} %bitcast.7, f32[32,16,128]{2,1,0:T(8,128)} %bitcast.8), custom_call_target="tpu_custom_call" | custom-call | tf_op jit(solution)/shard_map/assimilate/pallas_call | solution.py:482
  50.4 1.1 %settle.1 = bf16[20,32768]{1,0:T(8,128)(2,1)} custom-call(bf16[16,32768]{1,0:T(8,128)(2,1)S(1)} %get-tuple-element.7.o16_ref, bf16[4,32768]{1,0:T(4,128)(2,1)S(1)} %get-tuple-element.8.o4_ref), custom_call_target="tpu_custom_call" | custom-call | tf_op jit(solution)/shard_map/settle/pallas_call | solution.py:540

commit v8 on v7

--- a/solution.py
+++ b/solution.py
@@ -124,7 +124,8 @@
     for d in range(1, nm):
         pl.semaphore_signal(barrier, inc=1, device_id=along(d), device_id_type=MESH)
 
-    def greet(d, carry):
+    def greet(n, carry):
+        d = 1 + lax.rem(n + 8, ns - 1)
         pl.semaphore_signal(barrier, inc=1, device_id=plane(d), device_id_type=MESH)
         return carry
 
@@ -283,7 +284,8 @@
         tail = jnp.where(eight < 5, p1, pltpu.roll(p2, 2, 0))
         pk[o] = jnp.where(spot < 96, main, jnp.concatenate([head, tail], axis=0)).astype(BF16)
 
-    def send(d, carry):
+    def send(n, carry):
+        d = 1 + lax.rem(n + 8, ns - 1)
         pltpu.make_async_remote_copy(
             pk.at[lax.rem(me + d, ns)], rx.at[me], ps.at[0], pr.at[0],
             device_id=plane(d), device_id_type=MESH).start()
@@ -354,13 +356,13 @@
         weight = jnp.concatenate([va[h : h + 1], va[h + 8 : h + 9]], axis=1)
         ybar = jnp.sum(x, axis=0, keepdims=True) / members
         dev = x - ybar
-        cut = slice(h * 2 * LANES, (h + 1) * 2 * LANES)
-        an[:members, cut] = dev
-        an[members:, cut] = jnp.where(
-            iota((LANES - members, 2 * LANES), 0) == 0, seen - ybar, 0.0
-        )
-        wa[:, cut] = dev * weight
-    gr[...] = nt(wa[...], an[...], lax.Precision.HIGHEST).reshape(nown, chunk, LANES)
+        cut = [slice((t * 8 + h) * 2 * LANES, (t * 8 + h + 1) * 2 * LANES) for t in range(3)]
+        last = jnp.where(iota((LANES - members, 2 * LANES), 0) == 0, seen - ybar, 0.0)
+        high, low = split(jnp.concatenate([dev, last], axis=0))
+        an[:, cut[0]], an[:, cut[1]], an[:, cut[2]] = high, high, low
+        high, low = split(dev * weight)
+        wa[:, cut[0]], wa[:, cut[1]], wa[:, cut[2]] = high, low, high
+    gr[...] = nt(wa[...], an[...]).reshape(nown, chunk, LANES)
 
     mine = me // stride
     owns = jnp.logical_and(lax.rem(me, stride) == 0, mine < nown)
@@ -379,14 +381,16 @@
         def _():
             to_owner(i).start()
 
+    q = iota((members, LANES), 0)
+    slot = jnp.where(q < 16 * nm, q // 16, (q - 16 * nm) // (own - 16))
+    inner = jnp.where(q < 16 * nm, q % 16, 16 + (q - 16 * nm) % (own - 16))
+    dist = jnp.where(slot == 0, 0, jnp.where(slot == 1, nm - 1, slot - 1))
+    tab[:members, :LANES] = onehot(iota((members, LANES), 1) == (z + dist) % nm * own + inner).astype(BF16)
+
     for c in full_up0 + full_dn1:
         c.wait_recv()
     for c in wave3:
         c.start()
-    for c in near_up + near_dn + pass_up + pass_dn:
-        c.wait_recv()
-    x4[:, :qc] = jnp.concatenate([e4[:, pl.ds(mid, qc)]] + [q4[r] for r in range(3)], axis=0)
-
     @pl.when(owns)
     def _():
         rbuf[me] = gr[mine]
@@ -400,6 +404,13 @@
             return carry
 
         lax.fori_loop(1, ns, send_one, 0)
+
+    for c in near_up + near_dn + pass_up + pass_dn:
+        c.wait_recv()
+    x4[:, :qc] = jnp.concatenate([e4[:, pl.ds(mid, qc)]] + [q4[r] for r in range(3)], axis=0)
+
+    @pl.when(owns)
+    def _():
         tiles_moved(nown - 1, gs, gs, s2.at[0], r2.at[0]).wait_recv()
 
     @pl.when(jnp.logical_not(owns))
@@ -408,11 +419,6 @@
 
     mixing = transform(gs[...].reshape(members, LANES), members, yref, zref).astype(BF16)
 
-    q = iota((members, LANES), 0)
-    slot = jnp.where(q < 16 * nm, q // 16, (q - 16 * nm) // (own - 16))
-    inner = jnp.where(q < 16 * nm, q % 16, 16 + (q - 16 * nm) % (own - 16))
-    dist = jnp.where(slot == 0, 0, jnp.where(slot == 1, nm - 1, slot - 1))
-    tab[:members, :LANES] = onehot(iota((members, LANES), 1) == (z + dist) % nm * own + inner).astype(BF16)
     padded = jnp.concatenate([mixing, jnp.zeros((LANES - members, LANES), BF16)], axis=0)
     turned = nt(tab[:members, :LANES], padded).astype(BF16)
     mixp[...] = nt(turned, tab[:members, :LANES]).astype(BF16)
@@ -516,8 +522,8 @@
             pltpu.VMEM((own * 8, 2 * LANES), F32),
             pltpu.VMEM((nm, own * 8, 2 * LANES), BF16),
             pltpu.VMEM((2 * members * 8, LANES), F32),
-            pltpu.VMEM((LANES, share), F32),
-            pltpu.VMEM((members, share), F32),
+            pltpu.VMEM((LANES, 3 * share), BF16),
+            pltpu.VMEM((members, 3 * share), BF16),
             pltpu.VMEM((nown, members // nown, LANES), F32),
             pltpu.VMEM((ns, members // nown, LANES), F32),
             pltpu.VMEM((nown, members // nown, LANES), F32),

time: 51.6 us -> 51.9 us (level)
  no operation moved by 1% of the time
where the time goes in v8:
time: 51.9 us; the launch traced here: 51.8 us
  Pallas kernels  51.8 us (100%)
    pallas_call x1, Pallas kernels, per_device(): pl.pallas_call(functools.partial(kernel, ns, nm, own, tiles, slots, share...  50.7 us
    pallas_call x1, Pallas kernels, per_device(): pl.pallas_call(settle, out_shape=jax.ShapeDtypeStruct((own, cells), BF16)...  1.07 us

profile of v8, /device:TPU:1, one launch (start us, length us, event | category | flops | bytes accessed | tf_op | source)
XLA Modules:
  0.0 51.8 jit_solution(12951268174152516541)
XLA Ops:
  0.0 50.7 %assimilate.1 = (bf16[16,32768]{1,0:T(8,128)(2,1)S(1)}, bf16[4,32768]{1,0:T(4,128)(2,1)S(1)}) custom-call(bf16[20,32768]{1,0:T(8,128)(2,1)} %ens.1, bf16[12,16,16,128]{3,2,1,0:T(8,128)(2,1)} %bitcast.6, s32[12,256]{1,0:T(8,128)} %bitcast.9, f32[32,16,128]{2,1,0:T(8,128)} %bitcast.7, f32[32,16,128]{2,1,0:T(8,128)} %bitcast.8), custom_call_target="tpu_custom_call" | custom-call | tf_op jit(solution)/shard_map/assimilate/pallas_call | solution.py:488
  50.7 1.1 %settle.1 = bf16[20,32768]{1,0:T(8,128)(2,1)} custom-call(bf16[16,32768]{1,0:T(8,128)(2,1)S(1)} %get-tuple-element.7.o16_ref, bf16[4,32768]{1,0:T(4,128)(2,1)S(1)} %get-tuple-element.8.o4_ref), custom_call_target="tpu_custom_call" | custom-call | tf_op jit(solution)/shard_map/settle/pallas_call | solution.py:546
